TPU v7x, 32 devices: a whole 2x2x4 slice. The times are simulated.
32 devices in a mesh: bin: 4 (over x, core), fsdp: 8 (over z, y).
Axes of the slice: x: 2, y: 2, z: 4, core: 2. Of those that a mesh axis runs over, the one named last changes fastest.
Arguments:
- latents: bfloat16 [4, 16, 256, 1152], P('bin', 'fsdp'), may hold values from -6 to 6
- cond: float32 [4, 1152], P('bin'), may hold values from -6 to 6
- live: int32 [4, 8], P('bin', 'fsdp'), may hold values from 1 to 2, 12 in all within a row
- w_ada: bfloat16 [1152, 6912], P(None, 'fsdp'), may hold values from -0.375 to 0.375
- b_ada: bfloat16 [6912], P('fsdp'), may hold values from -3 to 3
- w_qkv: bfloat16 [1152, 3456], P('fsdp'), may hold values from -0.1875 to 0.1875
- b_qv: bfloat16 [2304], P('fsdp'), may hold values from -3 to 3
- w_proj: bfloat16 [1152, 1152], P('fsdp'), may hold values from -0.5 to 0.5
- b_proj: bfloat16 [1152], P('fsdp'), may hold values from -3 to 3
- w_fc1: bfloat16 [1152, 4608], P('fsdp'), may hold values from -0.1875 to 0.1875
- b_fc1: bfloat16 [4608], P('fsdp'), may hold values from -3 to 3
- w_fc2: bfloat16 [4608, 1152], P('fsdp'), may hold values from -0.09375 to 0.09375
- b_fc2: bfloat16 [1152], P('fsdp'), may hold values from -3 to 3
- cotangent: bfloat16 [4, 16, 256, 1152], P('bin', 'fsdp'), may hold values from -6 to 6
Outputs:
- block_out: bfloat16 [4, 16, 256, 1152], P('bin', 'fsdp')
- latents_grad: float32 [4, 16, 256, 1152], P('bin', 'fsdp')
- cond_grad: float32 [4, 1152], P('bin')
- w_ada_grad: float32 [1152, 6912], P(None, 'fsdp')
- b_ada_grad: float32 [6912], P('fsdp')
- w_qkv_grad: float32 [1152, 3456], P('fsdp')
- b_qv_grad: float32 [2304], P('fsdp')
- w_proj_grad: float32 [1152, 1152], P('fsdp')
- b_proj_grad: float32 [1152], P('fsdp')
- w_fc1_grad: float32 [1152, 4608], P('fsdp')
- b_fc1_grad: float32 [4608], P('fsdp')
- w_fc2_grad: float32 [4608, 1152], P('fsdp')
- b_fc2_grad: float32 [1152], P('fsdp')
Inputs may be any that keep to these rules, and one draw needn't show every extreme that they name: The counts of one bin's devices sum to 12; every bin has a device with 2 live images; a device's live images are its first slots.
All inputs are finite; a program needn't handle non-finite values.
Results may differ from a plain program's by a relative error of at most 0.015.
The roundings to bfloat16 on the way count: a program that leaves them out, or rounds other values in their place, can miss the bound.
Values may be sent and summed in bfloat16 or wider, within the bound.
A program may use at most 256 MiB of HBM per device.

v0:
```python
import jax
import jax.numpy as jnp
from jax import lax
from jax.sharding import PartitionSpec as P

HEAD_DIM = 72


def layer_norm(field):
    center = field - jnp.mean(field, axis=-1, keepdims=True)
    return center * lax.rsqrt(jnp.mean(center * center, axis=-1, keepdims=True) + 1e-06)


def gelu_tanh(field):
    return (
        0.5
        * field
        * (1.0 + jnp.tanh(0.7978845608028654 * (field + 0.044715 * field * field * field)))
    )


def modulate(field, shift_vec, scale_vec):
    return layer_norm(field) * (1.0 + scale_vec) + shift_vec


def pair_scores(query_block, key_block):
    return jnp.einsum(
        "gqhd,gkhd->ghqk", query_block, key_block, preferred_element_type=jnp.float32
    ) * HEAD_DIM ** (-0.5)


def attend_pair(group_item):
    query_block, key_block, value_block = group_item
    scores = pair_scores(query_block, key_block)
    highest = jnp.max(scores, axis=-1, keepdims=True)
    exp_scores = jnp.exp(scores - highest)
    totals = jnp.sum(exp_scores, axis=-1, keepdims=True)
    attn_probs = (exp_scores / totals).astype(jnp.bfloat16)
    attended = jnp.einsum(
        "ghqk,gkhd->gqhd", attn_probs, value_block, preferred_element_type=jnp.float32
    )
    return (attended, (highest + jnp.log(totals))[..., 0])


def attend_back(group_item):
    query_block, key_block, value_block, log_total, grad_att = group_item
    scores = pair_scores(query_block, key_block)
    attn_probs = jnp.exp(scores - log_total[..., None])
    grad_probs = jnp.einsum(
        "gqhd,gkhd->ghqk", grad_att, value_block, preferred_element_type=jnp.float32
    )
    row_terms = jnp.sum(attn_probs * grad_probs, axis=-1, keepdims=True)
    grad_scores = (attn_probs * (grad_probs - row_terms)).astype(jnp.bfloat16)
    grad_query = jnp.einsum(
        "ghqk,gkhd->gqhd", grad_scores, key_block, preferred_element_type=jnp.float32
    ) * HEAD_DIM ** (-0.5)
    grad_key = jnp.einsum(
        "ghqk,gqhd->gkhd", grad_scores, query_block, preferred_element_type=jnp.float32
    ) * HEAD_DIM ** (-0.5)
    grad_value = jnp.einsum(
        "ghqk,gqhd->gkhd",
        attn_probs.astype(jnp.bfloat16),
        grad_att,
        preferred_element_type=jnp.float32,
    )
    return jnp.stack([grad_query, grad_key, grad_value], axis=2)


def run_block(flat_rows, modulation, weights, images, length):
    full_qkv, full_proj, full_fc1, full_fc2, bias_qv, bias_proj, bias_fc1, bias_fc2 = weights
    width = flat_rows.shape[1]
    heads = width // HEAD_DIM
    pieces = jnp.split(modulation, 6)
    h_first = modulate(flat_rows, pieces[0], pieces[1]).astype(jnp.bfloat16)
    qkv_bias = jnp.concatenate(
        [bias_qv[:width], jnp.zeros((width,), jnp.bfloat16), bias_qv[width:]]
    ).astype(jnp.float32)
    qkv_rows = (jnp.dot(h_first, full_qkv, preferred_element_type=jnp.float32) + qkv_bias).astype(
        jnp.bfloat16
    )
    split_rows = qkv_rows.reshape(images // 2, 2, length, 3, heads, HEAD_DIM)
    attended, log_total = lax.map(
        attend_pair, (split_rows[:, :, :, 0], split_rows[:, :, :, 1], split_rows[:, :, :, 2])
    )
    attended = attended.reshape(images * length, width).astype(jnp.bfloat16)
    branch = jnp.dot(attended, full_proj, preferred_element_type=jnp.float32) + bias_proj.astype(
        jnp.float32
    )
    middle = flat_rows + pieces[2] * branch
    h_second = modulate(middle, pieces[3], pieces[4]).astype(jnp.bfloat16)
    pre_act = jnp.dot(h_second, full_fc1, preferred_element_type=jnp.float32) + bias_fc1.astype(
        jnp.float32
    )
    hidden = gelu_tanh(pre_act).astype(jnp.bfloat16)
    mlp_out = jnp.dot(hidden, full_fc2, preferred_element_type=jnp.float32) + bias_fc2.astype(
        jnp.float32
    )
    result = middle + pieces[5] * mlp_out
    return (
        h_first,
        split_rows,
        log_total,
        attended,
        branch,
        middle,
        h_second,
        pre_act,
        hidden,
        mlp_out,
        result,
    )


def on_device(
    latents,
    cond,
    live,
    w_ada,
    b_ada,
    w_qkv,
    b_qv,
    w_proj,
    b_proj,
    w_fc1,
    b_fc1,
    w_fc2,
    b_fc2,
    cotangent,
):
    images = latents.shape[1]
    length = latents.shape[2]
    width = latents.shape[3]
    heads = width // HEAD_DIM
    scaled = jax.nn.silu(cond[0]).astype(jnp.bfloat16)
    mod_part = jnp.dot(scaled, w_ada, preferred_element_type=jnp.float32) + b_ada.astype(
        jnp.float32
    )
    modulation = lax.all_gather(mod_part, "fsdp", axis=0, tiled=True)
    gathered = (
        lax.all_gather(w_qkv, "fsdp", axis=0, tiled=True),
        lax.all_gather(w_proj, "fsdp", axis=0, tiled=True),
        lax.all_gather(w_fc1, "fsdp", axis=0, tiled=True),
        lax.all_gather(w_fc2, "fsdp", axis=0, tiled=True),
        lax.all_gather(b_qv, "fsdp", axis=0, tiled=True),
        lax.all_gather(b_proj, "fsdp", axis=0, tiled=True),
        lax.all_gather(b_fc1, "fsdp", axis=0, tiled=True),
        lax.all_gather(b_fc2, "fsdp", axis=0, tiled=True),
    )
    flat_rows = latents[0].reshape(images * length, width).astype(jnp.float32)
    live_mask = (lax.iota(jnp.int32, images) < live[0, 0]).astype(jnp.float32)
    row_mask = jnp.repeat(live_mask, length)[:, None]
    forward_run = run_block(flat_rows, modulation, gathered, images, length)
    block_out = (forward_run[10] * row_mask).astype(jnp.bfloat16).reshape(latents.shape)
    weights = (
        lax.all_gather(w_qkv, "fsdp", axis=0, tiled=True),
        lax.all_gather(w_proj, "fsdp", axis=0, tiled=True),
        lax.all_gather(w_fc1, "fsdp", axis=0, tiled=True),
        lax.all_gather(w_fc2, "fsdp", axis=0, tiled=True),
        lax.all_gather(b_qv, "fsdp", axis=0, tiled=True),
        lax.all_gather(b_proj, "fsdp", axis=0, tiled=True),
        lax.all_gather(b_fc1, "fsdp", axis=0, tiled=True),
        lax.all_gather(b_fc2, "fsdp", axis=0, tiled=True),
    )
    full_qkv, full_proj, full_fc1, full_fc2 = (weights[0], weights[1], weights[2], weights[3])
    saved = run_block(flat_rows, modulation, weights, images, length)
    (
        h_first,
        split_rows,
        log_total,
        attended,
        branch,
        middle,
        h_second,
        pre_act,
        hidden,
        mlp_out,
        result,
    ) = saved
    pieces = jnp.split(modulation, 6)
    grad_res = cotangent[0].reshape(images * length, width).astype(jnp.float32) * row_mask
    grad_out = (pieces[5] * grad_res).astype(jnp.bfloat16)
    grad_gate_two = jnp.sum(grad_res * mlp_out, axis=0)
    grad_fc2 = jnp.einsum("rf,rd->fd", hidden, grad_out, preferred_element_type=jnp.float32)
    grad_bfc2 = jnp.sum(grad_out.astype(jnp.float32), axis=0)
    grad_hidden = jnp.einsum("rd,fd->rf", grad_out, full_fc2, preferred_element_type=jnp.float32)
    gelu_pull = jax.vjp(gelu_tanh, pre_act)[1]
    grad_pre = gelu_pull(grad_hidden)[0].astype(jnp.bfloat16)
    grad_fc1 = jnp.einsum("rd,rf->df", h_second, grad_pre, preferred_element_type=jnp.float32)
    grad_bfc1 = jnp.sum(grad_pre.astype(jnp.float32), axis=0)
    grad_h2 = jnp.einsum("rf,df->rd", grad_pre, full_fc1, preferred_element_type=jnp.float32)
    second_pull = jax.vjp(modulate, middle, pieces[3], pieces[4])[1]
    grad_mid_norm, grad_shift_two, grad_scale_two = second_pull(grad_h2)
    grad_mid = grad_res + grad_mid_norm
    grad_branch = (pieces[2] * grad_mid).astype(jnp.bfloat16)
    grad_gate_one = jnp.sum(grad_mid * branch, axis=0)
    grad_proj = jnp.einsum("rd,re->de", attended, grad_branch, preferred_element_type=jnp.float32)
    grad_bproj = jnp.sum(grad_branch.astype(jnp.float32), axis=0)
    grad_att = jnp.einsum(
        "re,de->rd", grad_branch, full_proj, preferred_element_type=jnp.float32
    ).astype(jnp.bfloat16)
    grad_att = grad_att.reshape(images // 2, 2, length, heads, HEAD_DIM)
    grad_qkv = lax.map(
        attend_back,
        (
            split_rows[:, :, :, 0],
            split_rows[:, :, :, 1],
            split_rows[:, :, :, 2],
            log_total,
            grad_att,
        ),
    )
    grad_qkv = grad_qkv.reshape(images * length, 3 * width).astype(jnp.bfloat16)
    grad_wqkv = jnp.einsum("rd,re->de", h_first, grad_qkv, preferred_element_type=jnp.float32)
    qkv_sums = jnp.sum(grad_qkv.astype(jnp.float32), axis=0)
    grad_bqv = jnp.concatenate([qkv_sums[:width], qkv_sums[2 * width :]])
    grad_h1 = jnp.einsum("re,de->rd", grad_qkv, full_qkv, preferred_element_type=jnp.float32)
    first_pull = jax.vjp(modulate, flat_rows, pieces[0], pieces[1])[1]
    grad_rows_norm, grad_shift_one, grad_scale_one = first_pull(grad_h1)
    grad_rows = grad_mid + grad_rows_norm
    grad_mod = jnp.concatenate(
        [
            grad_shift_one,
            grad_scale_one,
            grad_gate_one,
            grad_shift_two,
            grad_scale_two,
            grad_gate_two,
        ]
    )
    shards = (
        lax.psum_scatter(grad_wqkv, "fsdp", scatter_dimension=0, tiled=True),
        lax.psum_scatter(grad_proj, "fsdp", scatter_dimension=0, tiled=True),
        lax.psum_scatter(grad_fc1, "fsdp", scatter_dimension=0, tiled=True),
        lax.psum_scatter(grad_fc2, "fsdp", scatter_dimension=0, tiled=True),
        lax.psum_scatter(grad_bqv, "fsdp", scatter_dimension=0, tiled=True),
        lax.psum_scatter(grad_bproj, "fsdp", scatter_dimension=0, tiled=True),
        lax.psum_scatter(grad_bfc1, "fsdp", scatter_dimension=0, tiled=True),
        lax.psum_scatter(grad_bfc2, "fsdp", scatter_dimension=0, tiled=True),
        lax.psum_scatter(grad_mod, "fsdp", scatter_dimension=0, tiled=True),
    )
    mod_mine = shards[8]
    grad_wada = scaled.astype(jnp.float32)[:, None] * mod_mine[None, :]
    grad_scaled = jnp.dot(w_ada.astype(jnp.float32), mod_mine, precision=lax.Precision.HIGHEST)
    grad_scaled = lax.psum(grad_scaled, "fsdp")
    silu_pull = jax.vjp(jax.nn.silu, cond[0])[1]
    grad_cond = silu_pull(grad_scaled)[0][None, :]
    totals = lax.psum(
        (
            shards[0],
            shards[1],
            shards[2],
            shards[3],
            shards[4],
            shards[5],
            shards[6],
            shards[7],
            grad_wada,
            mod_mine,
        ),
        "bin",
    )
    return (
        block_out,
        grad_rows.reshape(latents.shape),
        grad_cond,
        totals[8],
        totals[9],
        totals[0],
        totals[4],
        totals[1],
        totals[5],
        totals[2],
        totals[6],
        totals[3],
        totals[7],
    )


def solution(mesh):
    return jax.shard_map(
        on_device,
        mesh=mesh,
        in_specs=(
            P("bin", "fsdp", None, None),
            P("bin", None),
            P("bin", "fsdp"),
            P(None, "fsdp"),
            P("fsdp"),
            P("fsdp", None),
            P("fsdp"),
            P("fsdp", None),
            P("fsdp"),
            P("fsdp", None),
            P("fsdp"),
            P("fsdp", None),
            P("fsdp"),
            P("bin", "fsdp", None, None),
        ),
        out_specs=(
            P("bin", "fsdp", None, None),
            P("bin", "fsdp", None, None),
            P("bin", None),
            P(None, "fsdp"),
            P("fsdp"),
            P("fsdp", None),
            P("fsdp"),
            P("fsdp", None),
            P("fsdp"),
            P("fsdp", None),
            P("fsdp"),
            P("fsdp", None),
            P("fsdp"),
        ),
        check_vma=False,
    )
```

profile of v0, /device:TPU:0, one launch (start us, length us, event | category | flops | bytes accessed | tf_op | source)
XLA Modules:
  0.0 1843.4 jit_solution(338678586922015093)
XLA Ops:
  16.1 40.7 %all-reduce.13 = (bf16[2304]{0:T(1024)(128)(2,1)S(1)}, bf16[1152]{0:T(1024)(128)(2,1)S(1)}, bf16[1152]{0:T(1024)(128)(2,1)}, bf16[4608]{0:T(1024)(128)(2,1)S(1)}) all-reduce(bf16[2304]{0:T(1024)(128)(2,1)S(1)} %dynamic-update-slice.1, bf16[1152]{0:T(1024)(128)(2,1)S(1)} %dynamic-update-slice.2, ...), channel_id=1, replica_groups=mesh['bin'=4,'fsdp'=8] {'fsdp'}, use_global_device_ids=true, to_apply=%add.1 | all-reduce | flops 9216 | bytes 36864
  58.9 34.3 %all-reduce = f32[6912]{0:T(1024)S(1)} all-reduce(f32[6912]{0:T(1024)S(1)} %add_dynamic-update-slice_fusion), channel_id=1, replica_groups=mesh['bin'=4,'fsdp'=8] {'fsdp'}, use_global_device_ids=true, to_apply=%add | all-reduce | flops 6912 | bytes 55296
  97.5 36.5 %all-gather.5.cloned.1.call-done = bf16[1152,3456]{1,0:T(8,128)(2,1)} async-done(((bf16[144,3456]{1,0:T(8,128)(2,1)}), bf16[1152,3456]{1,0:T(8,128)(2,1)}) %all-gather.5.cloned.1.call-update) | async-done | bytes 7962640 | tf_op jit(solution)/shard_map/all_gather | solution.py:140
  134.1 10.3 add_convert_fusion
  144.4 13.6 reshape.274
  157.9 6.0 fusion.57
  196.9 145.9 %all-gather.9.cloned.1.call-done = bf16[1152,4608]{1,0:T(8,128)(2,1)} async-done(((bf16[144,4608]{1,0:T(8,128)(2,1)}), bf16[1152,4608]{1,0:T(8,128)(2,1)}) %all-gather.9.cloned.1.call-update) | async-done | bytes 10616848 | tf_op jit(solution)/shard_map/all_gather | solution.py:142
  342.8 12.2 fusion.51
  355.0 140.5 %all-gather.11.cloned.1.call-done = bf16[4608,1152]{1,0:T(8,128)(2,1)} async-done(((bf16[576,1152]{1,0:T(8,128)(2,1)}), bf16[4608,1152]{1,0:T(8,128)(2,1)}) %all-gather.11.cloned.1.call-update) | async-done | bytes 10616848 | tf_op jit(solution)/shard_map/all_gather | solution.py:143
  495.5 18.9 %convert_reduce_fusion = (f32[4608]{0:T(1024)S(1)}, bf16[512,4608]{1,0:T(8,128)(2,1)}) fusion(f32[512,4608]{1,0:T(8,128)} %fusion.51, f32[4608]{0:T(1024)S(1)} %convert_element_type.166, bf16[512,1152]{1,0:T(8,128)(2,1)} %multiply_convert_fusion.4, bf16[4608,1152]{1,0:T(8,128)(2,1)} %all-gather.11.cloned.1.call-done), kind=kOutput, calls=%fused_computation.10 | convolution fusion | flops 5499514368 | bytes 25989120 | tf_op jit(solution)/shard_map/rd,fd->rf/dot_general | solution.py:185
  514.3 11.6 multiply_reduce_fusion.3
  549.5 6.7 multiply_reduce_fusion
  572.8 7.9 fusion.62
  580.8 13.0 fusion.50
  593.8 15.0 fusion.52
  610.2 9.9 fusion.27
  622.1 15.4 multiply_reduce_fusion.2
  637.6 36.1 %all-reduce.5 = f32[6912]{0:T(1024)S(1)} all-reduce(f32[6912]{0:T(1024)S(1)} %constant_dynamic-update-slice_fusion), channel_id=2, replica_groups=mesh['bin'=4,'fsdp'=8] {'fsdp'}, use_global_device_ids=true, to_apply=%region_17.18.clone | all-reduce | flops 6912 | bytes 55296
  676.0 232.5 %reduce-scatter.5.cloned.1.call-done = f32[144,3456]{1,0:T(8,128)} async-done(((f32[1152,3456]{1,0:T(8,128)}), f32[144,3456]{1,0:T(8,128)}) %reduce-scatter.5.cloned.1.call-update) | async-done | bytes 1990672 | tf_op jit(solution)/shard_map/reduce_scatter | solution.py:231
  908.5 350.7 %reduce-scatter.9.cloned.1.call-done = f32[144,4608]{1,0:T(8,128)} async-done(((f32[1152,4608]{1,0:T(8,128)}), f32[144,4608]{1,0:T(8,128)}) %reduce-scatter.9.cloned.1.call-update) | async-done | bytes 2654224 | tf_op jit(solution)/shard_map/reduce_scatter | solution.py:233
  1259.2 350.3 %reduce-scatter.11.cloned.1.call-done = f32[576,1152]{1,0:T(8,128)} async-done(((f32[4608,1152]{1,0:T(8,128)}), f32[576,1152]{1,0:T(8,128)}) %reduce-scatter.11.cloned.1.call-update) | async-done | bytes 2654224 | tf_op jit(solution)/shard_map/reduce_scatter | solution.py:234
  1613.1 35.7 %all-reduce.10 = (f32[1152]{0:T(1024)S(1)}, f32[2304]{0:T(1024)S(1)}, f32[1152]{0:T(1024)S(1)}, f32[4608]{0:T(1024)S(1)}, f32[1152]{0:T(1024)S(1)}) all-reduce(f32[1152]{0:T(1024)S(1)} %convolution_reduce_fusion, f32[2304]{0:T(1024)S(1)} %pad_maximum_fusion, ...), channel_id=1, replica_groups=mesh['bin'=4,'fsdp'=8] {'fsdp'}, use_global_device_ids=true, to_apply=%region_18.19 | all-reduce | flops 10368 | bytes 82944 | tf_op jit(solution)/shard_map/psum | solution.py:244
  1649.8 12.5 all-reduce.11
  1662.3 162.8 %all-reduce.16.cloned.1.call-done = (f32[1152,864]{0,1:T(8,128)}, f32[144,3456]{1,0:T(8,128)}, f32[144,1152]{1,0:T(8,128)}, f32[144,4608]{1,0:T(8,128)}, f32[576,1152]{1,0:T(8,128)}) async-done(((f32[1152,864]{0,1:T(8,128)}, f32[144,3456]{1,0:T(8,128)}, f32[144,1152]{1,0:T(8,128)}, f32[144,4608]{1,0:T(8,128)}, f32[576,1152]{1,0:T(8,128)}), (f32[1152,864]{0,1:T(8,128)}, f32[144,3456]{1,0:T(8,128)}, ...) | async-done | bytes 11943952 | tf_op jit(solution)/shard_map/psum | solution.py:247
  (210 shorter events, 103.9 us)
Async XLA Ops:
  7.2 51.0 %copy-start = (bf16[1152,864]{0,1:T(8,128)(2,1)S(1)}, bf16[1152,864]{0,1:T(8,128)(2,1)}, u32[]{:S(2)}) copy-start(bf16[1152,864]{0,1:T(8,128)(2,1)} %param.17) | copy-start | bytes 5971972
  7.2 8.7 copy-start.41
  7.3 49.6 %copy-start.2 = (bf16[1,2,256,1152]{3,2,1,0:T(8,128)(2,1)S(1)}, bf16[1,2,256,1152]{3,2,1,0:T(8,128)(2,1)}, u32[]{:S(2)}) copy-start(bf16[1,2,256,1152]{3,2,1,0:T(8,128)(2,1)} %param.14) | copy-start | bytes 3538948
  7.3 126.8 %all-gather.5.cloned.1.call-start = ((), (), s32[]{:S(2)}) async-start(), calls=%async_computation.4 | async-start | bytes 8957952 | tf_op jit(solution)/shard_map/all_gather | solution.py:140
  8.0 181.5 %all-gather.7.cloned.1.call-start = ((), (), s32[]{:S(2)}) async-start(), calls=%async_computation.5 | async-start | bytes 2985984 | tf_op jit(solution)/shard_map/all_gather | solution.py:141
  8.8 334.0 %all-gather.9.cloned.1.call-start = ((), (), s32[]{:S(2)}) async-start(), calls=%async_computation.6 | async-start | bytes 11943936 | tf_op jit(solution)/shard_map/all_gather | solution.py:142
  9.5 486.0 %all-gather.11.cloned.1.call-start = ((), (), s32[]{:S(2)}) async-start(), calls=%async_computation.7 | async-start | bytes 11943936 | tf_op jit(solution)/shard_map/all_gather | solution.py:143
  10.1 48.8 %copy-start.42 = (bf16[864]{0:T(1024)(128)(2,1)S(1)}, bf16[864]{0:T(1024)(128)(2,1)}, u32[]{:S(2)}) copy-start(bf16[864]{0:T(1024)(128)(2,1)} %param.18) | copy-start | bytes 5188
  10.1 666.0 %reduce-scatter.7.cloned.1.call-start = ((), (), s32[]{:S(2)}) async-start(), calls=%async_computation.9 | async-start | bytes 5971968 | tf_op jit(solution)/shard_map/reduce_scatter | solution.py:232
  11.3 82.0 %copy-start.27 = (f32[1152]{0:T(1024)}, f32[1152]{0:T(1024)S(1)}, u32[]{:S(2)}) copy-start(f32[1152]{0:T(1024)S(1)} %reduce.4) | copy-start | bytes 13828
  58.1 39.4 %copy-start.30 = (f32[512]{0:T(512)}, f32[512]{0:T(512)S(1)}, u32[]{:S(2)}) copy-start(f32[512]{0:T(512)S(1)} %rsqrt.27) | copy-start | bytes 6148
  58.1 39.4 %copy-start.32 = (f32[1,2,2,128]{3,1,2,0:T(2,128)}, f32[1,2,2,128]{3,1,2,0:T(2,128)S(1)}, u32[]{:S(2)}) copy-start(f32[1,2,2,128]{3,1,2,0:T(2,128)S(1)} %copy.73) | copy-start | bytes 6148
  495.5 18.9 %copy-start.4 = (f32[512,1152]{1,0:T(8,128)S(1)}, f32[512,1152]{1,0:T(8,128)}, u32[]{:S(2)}) copy-start(f32[512,1152]{1,0:T(8,128)} %copy-done.3) | copy-start | bytes 7077892
  533.2 375.3 %reduce-scatter.5.cloned.1.call-start = ((), (), s32[]{:S(2)}) async-start(), calls=%async_computation.8 | async-start | bytes 17915904 | tf_op jit(solution)/shard_map/reduce_scatter | solution.py:231
  549.5 13.8 slice-start
  580.7 678.5 %reduce-scatter.9.cloned.1.call-start = ((), (), s32[]{:S(2)}) async-start(), calls=%async_computation.10 | async-start | bytes 23887872 | tf_op jit(solution)/shard_map/reduce_scatter | solution.py:233
  593.8 1015.8 %reduce-scatter.11.cloned.1.call-start = ((), (), s32[]{:S(2)}) async-start(), calls=%async_computation.11 | async-start | bytes 23887872 | tf_op jit(solution)/shard_map/reduce_scatter | solution.py:234
  608.8 1216.3 %all-reduce.16.cloned.1.call-start = ((), (), s32[]{:S(2)}) async-start(), calls=%async_computation.12 | async-start | bytes 23887872 | tf_op jit(solution)/shard_map/psum | solution.py:247
  610.2 9.9 copy-start.35
  610.2 10.0 copy-start.31
  610.2 11.1 copy-start.13
  610.2 11.1 copy-start.19
  622.1 51.7 %copy-start.29 = (f32[1152]{0:T(1024)S(1)}, f32[1152]{0:T(1024)}, u32[]{:S(2)}) copy-start(f32[1152]{0:T(1024)} %get-tuple-element.94) | copy-start | bytes 13828
  1609.6 39.3 %copy-start.28 = (f32[1152]{0:T(1024)S(1)}, f32[1152]{0:T(1024)}, u32[]{:S(2)}) copy-start(f32[1152]{0:T(1024)} %copy-done.27) | copy-start | bytes 13828
  (33 other events, 96.3 us)
Sparse Core Ops, SparseCore 0:
  10.3 123.7 all-gather.4
  136.2 53.2 all-gather.6
  191.7 151.0 all-gather.8
  344.8 150.6 all-gather.10
  533.3 102.2 reduce-scatter.6
  639.8 268.6 reduce-scatter.4
  912.9 346.2 reduce-scatter.8
  1263.1 346.3 reduce-scatter.10
  1613.4 211.6 all-reduce.15
where the time goes:
time: 1850 us; the launch traced here: 1840 us
  waiting for transfers between devices  1420 us (77%)
  blocking collectives  159 us (9%)
  matrix products  146 us (8%)
  local copies, waits for them, and re-layouts  72.8 us (4%)
  between operations  20.7 us (1%)
  other arithmetic  20.4 us (1%)
    reduce_scatter x1, waiting for transfers between devices, on_device(): lax.psum_scatter(grad_fc1, 'fsdp', scatter_dimension=0, tiled=True)  351 us
    reduce_scatter x1, waiting for transfers between devices, on_device(): lax.psum_scatter(grad_fc2, 'fsdp', scatter_dimension=0, tiled=True)  350 us
    reduce_scatter x1, waiting for transfers between devices, on_device(): lax.psum_scatter(grad_wqkv, 'fsdp', scatter_dimension=0, tiled=True)  232 us
    psum x1, waiting for transfers between devices, on_device(): lax.psum((shards[0], shards[1], shards[2], shards[3], shards[4], shards[5...  163 us
    all_gather x1, waiting for transfers between devices, on_device(): lax.all_gather(w_fc1, 'fsdp', axis=0, tiled=True)  146 us
    all_gather x1, waiting for transfers between devices, on_device(): lax.all_gather(w_fc2, 'fsdp', axis=0, tiled=True)  140 us
    unnamed x3, blocking collectives  111 us
    unnamed x128, local copies, waits for them, and re-layouts  37.7 us
  transfers between devices with their start and end apart: 9, of which 8 were waited for; matrix products, arithmetic and copies ran while one was open for 10% of the time, Pallas kernels for 0%

commit v1 on v0

--- a/solution.py
+++ b/solution.py
@@ -1,9 +1,17 @@
+import functools
+
 import jax
 import jax.numpy as jnp
 from jax import lax
+from jax.experimental import pallas as pl
+from jax.experimental.pallas import tpu as pltpu
 from jax.sharding import PartitionSpec as P
 
 HEAD_DIM = 72
+MESH = pl.DeviceIdType.MESH
+ROWS = 144
+WID = 1152
+NG = 3
 
 
 def layer_norm(field):
@@ -111,7 +119,7 @@
     )
 
 
-def on_device(
+def on_device_generic(
     latents,
     cond,
     live,
@@ -276,9 +284,479 @@
     )
 
 
+def coords():
+    b=lax.axis_index("bin"); f=lax.axis_index("fsdp")
+    x=b//2; c=lax.rem(b,2); z=f//2; y=lax.rem(f,2)
+    return b,f,x,c,z,y
+
+def gather_kernel(small_ref, la_ref, lb_ref, lc_ref, so_ref, wa_ref, wb_ref, wc_ref, loc_sem, sm_send, sm_recv, send_sem, recv_sem):
+    b,f,x,c,z,y=coords()
+    bx=lax.rem(b+2,4)
+    bc=b+1-2*c
+    bxc=lax.rem(bc+2,4)
+    fy=f+1-2*y
+    z1=z+1-2*lax.rem(z,2)
+    mid=jnp.logical_or(z==1,z==2)
+    zb=lax.rem(z+2,4)
+    zc=3-z
+    z2=jnp.where(mid,zc,zb); z3=jnp.where(mid,zb,zc)
+    bar=pltpu.get_barrier_semaphore()
+    for k in range(1,8):
+        pl.semaphore_signal(bar,inc=1,device_id=(b,lax.rem(f+k,8)),device_id_type=MESH)
+    pl.semaphore_signal(bar,inc=1,device_id=(bx,f),device_id_type=MESH)
+    pl.semaphore_signal(bar,inc=1,device_id=(bc,f),device_id_type=MESH)
+    pl.semaphore_wait(bar,9)
+    W=(wa_ref,wb_ref,wc_ref); L=(la_ref,lb_ref,lc_ref)
+    def blk(g,j,ff):
+        return W[g].at[j,ff] if g<2 else W[g].at[ff,j]
+    smalls=[]
+    for k in range(1,8):
+        cp=pltpu.make_async_remote_copy(src_ref=small_ref,dst_ref=so_ref.at[f],send_sem=sm_send.at[k],recv_sem=sm_recv.at[f],
+            device_id=(b,lax.rem(f+k,8)),device_id_type=MESH)
+        cp.start(); smalls.append(cp)
+    own=pltpu.make_async_copy(small_ref,so_ref.at[f],sm_send.at[0]); own.start()
+    locs=[]
+    for g in range(NG):
+        for j in range(4):
+            cp=pltpu.make_async_copy(L[g].at[j],blk(g,j,f),loc_sem.at[g,j]); cp.start(); locs.append(cp)
+    pend=[]
+    cnt=[0,0,0]
+    def send(g,j,ff,dev,cond=None,src=None):
+        i=cnt[g]; cnt[g]+=1
+        cp=pltpu.make_async_remote_copy(src_ref=blk(g,j,ff) if src is None else src,dst_ref=blk(g,j,ff),send_sem=send_sem.at[g,i],recv_sem=recv_sem.at[g,j,ff],device_id=dev,device_id_type=MESH)
+        if cond is None: cp.start()
+        else:
+            @pl.when(cond)
+            def _(): cp.start()
+        pend.append((cp,cond))
+    def arrive(g,j,ff):
+        pltpu.make_async_copy(blk(g,j,ff),blk(g,j,ff),recv_sem.at[g,j,ff]).wait()
+    up=(b,jnp.minimum(f+2,7)); dn=(b,jnp.maximum(f-2,0))
+    fz1=z1*2+y
+    def init(g):
+        sb=L[g].at[b]; sx=L[g].at[bx]
+        send(g,b,f,up,z<3,sb); send(g,b,f,dn,z>0,sb); send(g,b,f,(b,fy),None,sb); send(g,bx,f,(b,fz1),None,sx); send(g,bx,f,(b,fy),None,sx)
+    def Z(g,zz,x_too):
+        ff=zz*2+y
+        arrive(g,b,ff)
+        send(g,b,ff,up,jnp.logical_and(zz<z,z<3)); send(g,b,ff,dn,jnp.logical_and(zz>z,z>0))
+        send(g,b,ff,(b,fy))
+        if x_too: send(g,b,ff,(bx,f))
+        send(g,b,ff,(bc,f))
+    def Y(g,zz,x_too):
+        ff=zz*2+1-y
+        arrive(g,b,ff)
+        if x_too: send(g,b,ff,(bx,f))
+        send(g,b,ff,(bc,f))
+    def X(g,j,ff):
+        arrive(g,j,ff); send(g,j,ff,(bc,f))
+    acts=[]
+    for g in range(NG):
+        a=[lambda g=g: Z(g,z1,False), lambda g=g: X(g,bx,fz1), lambda g=g: Y(g,z,False), lambda g=g: X(g,bx,fy),
+           lambda g=g: Z(g,z2,True), lambda g=g: Y(g,z1,True), lambda g=g: Z(g,z3,True), lambda g=g: X(g,bx,z2*2+y), lambda g=g: Y(g,z2,True),
+           lambda g=g: X(g,bx,z1*2+1-y), lambda g=g: X(g,bx,z3*2+y), lambda g=g: Y(g,z3,True), lambda g=g: X(g,bx,z2*2+1-y), lambda g=g: X(g,bx,z3*2+1-y)]
+        acts.append(a)
+    init(0)
+    for g in range(NG):
+        for i,a in enumerate(acts[g]):
+            a()
+            if i==7 and g<NG-1: init(g+1)
+    for g in range(NG):
+        for zz in range(4):
+            for jj in (bc,bxc):
+                @pl.when(zz!=z)
+                def _(): arrive(g,jj,zz*2+y)
+                arrive(g,jj,zz*2+1-y)
+    for cp,cond in pend:
+        if cond is None: cp.wait_send()
+        else:
+            @pl.when(cond)
+            def _(cp=cp): cp.wait_send()
+    own.wait()
+    for cp in locs: cp.wait()
+    for cp in smalls: cp.wait_send()
+    for k in range(1,8):
+        ff=lax.rem(f+k,8)
+        pltpu.make_async_copy(so_ref.at[ff],so_ref.at[ff],sm_recv.at[ff]).wait()
+
+def gather(small,la,lb,lc):
+    A=pl.BlockSpec(memory_space=pl.ANY)
+    return pl.pallas_call(gather_kernel,
+        out_shape=(jax.ShapeDtypeStruct((8,8,256),jnp.float32),jax.ShapeDtypeStruct((4,8,ROWS,WID),jnp.bfloat16),jax.ShapeDtypeStruct((4,8,ROWS,WID),jnp.bfloat16),jax.ShapeDtypeStruct((8,4,ROWS,WID),jnp.bfloat16)),
+        in_specs=[A]+[pl.BlockSpec(memory_space=pltpu.VMEM)]*3,out_specs=(A,)*4,
+        scratch_shapes=[pltpu.SemaphoreType.DMA((3,4)),pltpu.SemaphoreType.DMA((8,)),pltpu.SemaphoreType.DMA((8,)),pltpu.SemaphoreType.DMA((3,40)),pltpu.SemaphoreType.DMA((3,4,8))],
+        compiler_params=pltpu.CompilerParams(collective_id=1,has_side_effects=True),name="gather_weights")(small,la,lb,lc)
+
+
+def reduce_kernel(small_ref, pa_ref, pb_ref, pc_ref, so_ref, oa_ref, ob_ref, oc_ref,
+                  t, r0, rx4, ry4, ry3, rx2, rn, rz, rt, fin,
+                  ld_sem, s0_send, s0_recv, send_sem, rx4_s, ry4_s, ry3_s, rx2_s, rn_s, rz_s, rt_s, o_loc, o_send, o_recv, sm_send, sm_recv):
+    b,f,x,c,z,y=coords()
+    bx=lax.rem(b+2,4); bc=b+1-2*c; bxc=lax.rem(bc+2,4)
+    fy=f+1-2*y; yb=1-y
+    z1=z+1-2*lax.rem(z,2)
+    mid=jnp.logical_or(z==1,z==2)
+    zb=lax.rem(z+2,4); zc=3-z
+    z2=jnp.where(mid,zc,zb); z3=jnp.where(mid,zb,zc)
+    fz1=z1*2+y
+    bar=pltpu.get_barrier_semaphore()
+    for k in range(1,32):
+        d=lax.rem(b*8+f+k,32)
+        pl.semaphore_signal(bar,inc=1,device_id=(d//8,lax.rem(d,8)),device_id_type=MESH)
+    pl.semaphore_wait(bar,31)
+    P=(pa_ref,pb_ref,pc_ref); O=(oa_ref,ob_ref,oc_ref)
+    def blk(g,j,ff):
+        return P[g].at[j,ff] if g<2 else P[g].at[ff,j]
+    tw=[]
+    order=[(1,z3,yb),(1,z2,yb),(1,z3,y),(1,z2,y),(1,z1,yb),(1,z,yb),(0,z3,yb),(0,z2,yb),(0,z1,yb),(0,z,yb),(0,z3,y),(0,z2,y),(1,z1,y),(0,z1,y),(0,z,y),(1,z,y)]
+    mine=(b,bx); his=(bc,bxc)
+    loads=[]
+    for g in range(NG):
+        for i,(jj,zz,yy) in enumerate(order):
+            ff=zz*2+yy
+            cp=pltpu.make_async_remote_copy(src_ref=blk(g,his[jj],ff),dst_ref=r0.at[g,i],send_sem=s0_send.at[g,i],recv_sem=s0_recv.at[g,i],device_id=(bc,f),device_id_type=MESH)
+            cp.start(); tw.append((cp,None))
+            ld=pltpu.make_async_copy(blk(g,mine[jj],ff),t.at[g,i],ld_sem.at[g,i]); ld.start(); loads.append(ld)
+    sms=[]
+    for k in range(1,32):
+        d=lax.rem(b*8+f+k,32)
+        cp=pltpu.make_async_remote_copy(src_ref=small_ref.at[lax.rem(d,8)],dst_ref=so_ref.at[b*8+f],send_sem=sm_send.at[k],recv_sem=sm_recv.at[b*8+f],device_id=(d//8,lax.rem(d,8)),device_id_type=MESH)
+        cp.start(); sms.append(cp)
+    own=pltpu.make_async_copy(small_ref.at[f],so_ref.at[b*8+f],sm_send.at[0]); own.start()
+    def wait_on(ref,sem): pltpu.make_async_copy(ref,ref,sem).wait()
+    def base(g,i):
+        loads[g*16+i].wait(); wait_on(r0.at[g,i],s0_recv.at[g,i])
+    def add(dst,srcs):
+        @pl.loop(0,ROWS//16)
+        def _(k):
+            rows=pl.ds(pl.multiple_of(k*16,16),16)
+            v=srcs[0][rows,:].astype(jnp.float32)
+            for s in srcs[1:]: v=v+s[rows,:].astype(jnp.float32)
+            dst[rows,:]=v.astype(dst.dtype)
+    cnt=[0]*3
+    def send(g,src,dst,rsem,dev,cond=None):
+        i=cnt[g]; cnt[g]+=1
+        cp=pltpu.make_async_remote_copy(src_ref=src,dst_ref=dst,send_sem=send_sem.at[g,i],recv_sem=rsem,device_id=dev,device_id_type=MESH)
+        if cond is None: cp.start()
+        else:
+            @pl.when(cond)
+            def _(): cp.start()
+        tw.append((cp,cond))
+    X=(bx,f); Y=(b,fy)
+    def a4x(g,i,slot):
+        base(g,i); add(t.at[g,i],[t.at[g,i],r0.at[g,i]]); send(g,t.at[g,i],rx4.at[g,slot],rx4_s.at[g,slot],X)
+    def a2(g,i,slot):
+        base(g,i); add(t.at[g,i],[t.at[g,i],r0.at[g,i]]); send(g,t.at[g,i],rx2.at[g,slot],rx2_s.at[g,slot],X)
+    def a4y(g,i,slot):
+        base(g,i); add(t.at[g,i],[t.at[g,i],r0.at[g,i]]); send(g,t.at[g,i],ry4.at[g,slot],ry4_s.at[g,slot],Y)
+    def a3(g,i,slot,rslot):
+        base(g,i)
+        s=[t.at[g,i],r0.at[g,i]]
+        if rslot is not None:
+            wait_on(rx4.at[g,rslot],rx4_s.at[g,rslot]); s.append(rx4.at[g,rslot])
+        add(t.at[g,i],s); send(g,t.at[g,i],ry3.at[g,slot],ry3_s.at[g,slot],Y)
+    def m(g,i,zz,rslot,yslot):
+        base(g,i)
+        s=[t.at[g,i],r0.at[g,i]]
+        if rslot is not None:
+            wait_on(rx2.at[g,rslot],rx2_s.at[g,rslot]); s.append(rx2.at[g,rslot])
+        wait_on(ry3.at[g,yslot],ry3_s.at[g,yslot]); s.append(ry3.at[g,yslot])
+        behind=jnp.where(zz>z,z>0,z<3)
+        add(t.at[g,i],s)
+        @pl.when(behind)
+        def _():
+            wait_on(rz.at[g,zz],rz_s.at[g,zz]); add(t.at[g,i],[t.at[g,i],rz.at[g,zz]])
+        nz=jnp.where(zz>z,z+1,z-1)
+        slot=jnp.where(jnp.logical_and(zz==nz,zz<z),4,zz)
+        send(g,t.at[g,i],rz.at[g,slot],rz_s.at[g,slot],(b,nz*2+y))
+    def n(g,i):
+        base(g,i); wait_on(ry4.at[g,1],ry4_s.at[g,1])
+        add(t.at[g,i],[t.at[g,i],r0.at[g,i],ry4.at[g,1]]); send(g,t.at[g,i],rn.at[g],rn_s.at[g],(b,fz1))
+    def t1(g,i):
+        base(g,i); wait_on(ry3.at[g,0],ry3_s.at[g,0])
+        add(t.at[g,i],[t.at[g,i],r0.at[g,i],ry3.at[g,0]])
+        @pl.when(z>0)
+        def _():
+            wait_on(rz.at[g,z],rz_s.at[g,z]); add(t.at[g,i],[t.at[g,i],rz.at[g,z]])
+        @pl.when(z<3)
+        def _():
+            wait_on(rz.at[g,4],rz_s.at[g,4]); add(t.at[g,i],[t.at[g,i],rz.at[g,4]])
+        send(g,t.at[g,i],rt.at[g,0],rt_s.at[g,0],X)
+    def t2(g,i):
+        base(g,i); wait_on(ry4.at[g,0],ry4_s.at[g,0]); wait_on(rn.at[g],rn_s.at[g])
+        add(t.at[g,i],[t.at[g,i],r0.at[g,i],ry4.at[g,0],rn.at[g]])
+        send(g,t.at[g,i],rt.at[g,1],rt_s.at[g,1],X)
+    def final(g):
+        for q,(i,slot,j) in enumerate(((14,1,b),(15,0,bx))):
+            wait_on(rt.at[g,slot],rt_s.at[g,slot])
+            add(fin.at[g,q],[t.at[g,i],rt.at[g,slot]])
+            cp=pltpu.make_async_copy(fin.at[g,q],O[g].at[j],o_loc.at[g,q]); cp.start()
+            rc=pltpu.make_async_remote_copy(src_ref=fin.at[g,q],dst_ref=O[g].at[j],send_sem=o_send.at[g,q],recv_sem=o_recv.at[g,q],device_id=(bc,f),device_id_type=MESH)
+            rc.start(); tw.append((rc,None)); loads2.append(cp)
+    loads2=[]
+    acts=[]
+    for g in range(NG):
+        a=[lambda g=g: a4x(g,0,0), lambda g=g: a4x(g,1,1), lambda g=g: a2(g,2,0), lambda g=g: a4y(g,4,1), lambda g=g: a2(g,3,1), lambda g=g: a4y(g,5,0),
+           lambda g=g: a3(g,8,1,None), lambda g=g: a3(g,6,3,0), lambda g=g: a3(g,7,2,1), lambda g=g: a3(g,9,0,None)]
+        e=[lambda g=g: m(g,10,z3,0,3), lambda g=g: m(g,11,z2,1,2), lambda g=g: n(g,12), lambda g=g: m(g,13,z1,None,1), lambda g=g: t2(g,15), lambda g=g: t1(g,14), lambda g=g: final(g)]
+        acts.append((a,e))
+    seq=list(acts[0][0])
+    for g in range(NG):
+        e=acts[g][1]; a=acts[g+1][0] if g+1<NG else []
+        k=max(len(e),len(a))
+        for i in range(k):
+            if i<len(a): seq.append(a[i])
+            if i<len(e): seq.append(e[i])
+    for s in seq: s()
+    for g in range(NG):
+        for q,j in enumerate((bc,bxc)):
+            wait_on(O[g].at[j],o_recv.at[g,q])
+    for cp,cond in tw:
+        if cond is None: cp.wait_send()
+        else:
+            @pl.when(cond)
+            def _(cp=cp): cp.wait_send()
+    for cp in loads2: cp.wait()
+    own.wait()
+    for cp in sms: cp.wait_send()
+    for k in range(1,32):
+        d=lax.rem(b*8+f+k,32)
+        wait_on(so_ref.at[d],sm_recv.at[d])
+
+def reduce(small,pa,pb,pc):
+    A=pl.BlockSpec(memory_space=pl.ANY)
+    D=pltpu.SemaphoreType.DMA
+    B=jnp.bfloat16
+    def V(*s,dt=B): return pltpu.VMEM(s+(ROWS,WID),dt)
+    return pl.pallas_call(reduce_kernel,
+        out_shape=(jax.ShapeDtypeStruct((32,8,256),jnp.float32),)+(jax.ShapeDtypeStruct((4,ROWS,WID),jnp.float32),)*3,
+        in_specs=[A]*4,out_specs=(A,)*4,
+        scratch_shapes=[V(3,16),V(3,16),V(3,2),V(3,2),V(3,4),V(3,2),V(3),V(3,5),V(3,2),V(3,2,dt=jnp.float32),
+           D((3,16)),D((3,16)),D((3,16)),D((3,24)),D((3,2)),D((3,2)),D((3,4)),D((3,2)),D((3,)),D((3,5)),D((3,2)),D((3,2)),D((3,2)),D((3,2)),D((32,)),D((32,))],
+        compiler_params=pltpu.CompilerParams(collective_id=2,has_side_effects=True,vmem_limit_bytes=63<<20),name="reduce_grads")(small,pa,pb,pc)
+
+
+def head_window(h):
+    start = HEAD_DIM * h
+    low = start // 128 * 128
+    width = 128 if start - low + HEAD_DIM <= 128 else 256
+    return low, width, start - low
+
+
+def attend_head(q, k, v, off, width):
+    lanes = lax.broadcasted_iota(jnp.int32, (1, width), 1)
+    keep = jnp.logical_and(lanes >= off, lanes < off + HEAD_DIM)
+    q = jnp.where(keep, q, jnp.zeros_like(q))
+    v = jnp.where(keep, v, jnp.zeros_like(v))
+    scores = lax.dot_general(k, q, (((1,), (1,)), ((), ())), preferred_element_type=jnp.float32)
+    scores = scores * HEAD_DIM ** (-0.5)
+    e = jnp.exp(scores - jnp.max(scores, axis=0, keepdims=True))
+    probs = e * (1.0 / jnp.sum(e, axis=0, keepdims=True))
+    return lax.dot_general(
+        probs.astype(jnp.bfloat16), v, (((0,), (0,)), ((), ())), preferred_element_type=jnp.float32
+    )
+
+
+def attend_kernel(q_ref, k_ref, v_ref, out_ref, acc):
+    acc[...] = jnp.zeros_like(acc)
+    for h in range(q_ref.shape[1] // HEAD_DIM):
+        low, width, off = head_window(h)
+        cols = slice(low, low + width)
+        acc[:, cols] += attend_head(q_ref[:, cols], k_ref[:, cols], v_ref[:, cols], off, width)
+    out_ref[...] = acc[...].astype(jnp.bfloat16)
+
+
+def attend(q, k, v, length):
+    rows, width = q.shape
+    spec = pl.BlockSpec((length, width), lambda i: (i, 0))
+    return pl.pallas_call(
+        attend_kernel,
+        grid=(rows // length,),
+        out_shape=jax.ShapeDtypeStruct((rows, width), jnp.bfloat16),
+        in_specs=[spec] * 3,
+        out_specs=spec,
+        scratch_shapes=[pltpu.VMEM((length, width), jnp.float32)],
+        compiler_params=pltpu.CompilerParams(vmem_limit_bytes=40 << 20),
+        name="attend",
+    )(q, k, v)
+
+
+def attend_head_back(q, k, v, g, off, width):
+    lanes = lax.broadcasted_iota(jnp.int32, (1, width), 1)
+    keep = jnp.logical_and(lanes >= off, lanes < off + HEAD_DIM)
+    q = jnp.where(keep, q, jnp.zeros_like(q))
+    g = jnp.where(keep, g, jnp.zeros_like(g))
+    k_own = jnp.where(keep, k, jnp.zeros_like(k))
+    nt = (((1,), (1,)), ((), ()))
+    scores = lax.dot_general(k, q, nt, preferred_element_type=jnp.float32) * HEAD_DIM ** (-0.5)
+    e = jnp.exp(scores - jnp.max(scores, axis=0, keepdims=True))
+    probs = e * (1.0 / jnp.sum(e, axis=0, keepdims=True))
+    grad_probs = lax.dot_general(v, g, nt, preferred_element_type=jnp.float32)
+    row = jnp.sum(probs * grad_probs, axis=0, keepdims=True)
+    grad_scores = (probs * (grad_probs - row)).astype(jnp.bfloat16)
+    grad_v = jnp.dot(probs.astype(jnp.bfloat16), g, preferred_element_type=jnp.float32)
+    grad_k = jnp.dot(grad_scores, q, preferred_element_type=jnp.float32) * HEAD_DIM ** (-0.5)
+    grad_q = lax.dot_general(
+        grad_scores, k_own, (((0,), (0,)), ((), ())), preferred_element_type=jnp.float32
+    ) * HEAD_DIM ** (-0.5)
+    return grad_q, grad_k, grad_v
+
+
+def attend_back_kernel(q_ref, k_ref, v_ref, g_ref, dq_ref, dk_ref, dv_ref, aq, ak, av):
+    for acc in (aq, ak, av):
+        acc[...] = jnp.zeros_like(acc)
+    for h in range(q_ref.shape[1] // HEAD_DIM):
+        low, width, off = head_window(h)
+        cols = slice(low, low + width)
+        out = attend_head_back(q_ref[:, cols], k_ref[:, cols], v_ref[:, cols], g_ref[:, cols], off, width)
+        for acc, part in zip((aq, ak, av), out):
+            acc[:, cols] += part
+    for ref, acc in zip((dq_ref, dk_ref, dv_ref), (aq, ak, av)):
+        ref[...] = acc[...].astype(jnp.bfloat16)
+
+
+def attend_grads(q, k, v, g, length):
+    rows, width = q.shape
+    spec = pl.BlockSpec((length, width), lambda i: (i, 0))
+    return pl.pallas_call(
+        attend_back_kernel,
+        grid=(rows // length,),
+        out_shape=(jax.ShapeDtypeStruct((rows, width), jnp.bfloat16),) * 3,
+        in_specs=[spec] * 4,
+        out_specs=(spec,) * 3,
+        scratch_shapes=[pltpu.VMEM((length, width), jnp.float32)] * 3,
+        compiler_params=pltpu.CompilerParams(vmem_limit_bytes=40 << 20),
+        name="attend_grads",
+    )(q, k, v, g)
+
+
+def on_device_fast(
+    latents, cond, live, w_ada, b_ada, w_qkv, b_qv, w_proj, b_proj, w_fc1, b_fc1, w_fc2, b_fc2, cotangent
+):
+    images, length, width = latents.shape[1:]
+    rows = images * length
+    f32 = jnp.float32
+    scaled = jax.nn.silu(cond[0]).astype(jnp.bfloat16)
+    mod_part = jnp.dot(scaled, w_ada, preferred_element_type=f32) + b_ada.astype(f32)
+    biases = jnp.concatenate([b_qv, b_proj, b_fc1, b_fc2]).astype(f32)
+    small = jnp.concatenate([mod_part, biases, jnp.zeros((32,), f32)]).reshape(8, 256)
+    la = jnp.concatenate([jnp.transpose(w_qkv.reshape(ROWS, 3, WID), (1, 0, 2)), w_proj[None]])
+    lb = jnp.transpose(w_fc1.reshape(ROWS, 4, WID), (1, 0, 2))
+    lc = w_fc2.reshape(4, ROWS, WID)
+    so, wa, wb, wc = gather(small, la, lb, lc)
+    so = so.reshape(8, 2048)
+    modulation = so[:, :864].reshape(6, width)
+    bias_qv = so[:, 864:1152].reshape(2, width)
+    bias_proj = so[:, 1152:1296].reshape(width)
+    bias_fc1 = so[:, 1296:1872].reshape(4 * width)
+    bias_fc2 = so[:, 1872:2016].reshape(width)
+    wa = wa.reshape(4, width, width)
+    wb = wb.reshape(4, width, width)
+    wc = wc.reshape(4 * width, width)
+    flat_rows = latents[0].reshape(rows, width).astype(f32)
+    live_mask = (lax.iota(jnp.int32, images) < live[0, 0]).astype(f32)
+    row_mask = jnp.repeat(live_mask, length)[:, None]
+    h_first = modulate(flat_rows, modulation[0], modulation[1]).astype(jnp.bfloat16)
+
+    def dense(left, right):
+        return jnp.dot(left, right, preferred_element_type=f32)
+
+    q = (dense(h_first, wa[0]) + bias_qv[0]).astype(jnp.bfloat16)
+    k = dense(h_first, wa[1]).astype(jnp.bfloat16)
+    v = (dense(h_first, wa[2]) + bias_qv[1]).astype(jnp.bfloat16)
+    attended = attend(q, k, v, length)
+    branch = dense(attended, wa[3]) + bias_proj
+    middle = flat_rows + modulation[2] * branch
+    h_second = modulate(middle, modulation[3], modulation[4]).astype(jnp.bfloat16)
+    pre = [dense(h_second, wb[j]) + bias_fc1[j * width : (j + 1) * width] for j in range(4)]
+    hidden = jnp.concatenate([gelu_tanh(p).astype(jnp.bfloat16) for p in pre], axis=1)
+    mlp_out = dense(hidden, wc) + bias_fc2
+    block_out = ((middle + modulation[5] * mlp_out) * row_mask).astype(jnp.bfloat16)
+    grad_res = cotangent[0].reshape(rows, width).astype(f32) * row_mask
+    grad_out = (modulation[5] * grad_res).astype(jnp.bfloat16)
+    grad_gate_two = jnp.sum(grad_res * mlp_out, axis=0)
+
+    def outer(left, right):
+        return jnp.einsum("rd,re->de", left, right, preferred_element_type=f32)
+
+    grad_fc2 = outer(hidden, grad_out).astype(jnp.bfloat16)
+    grad_bfc2 = jnp.sum(grad_out.astype(f32), axis=0)
+    grad_pre, grad_fc1 = [], []
+    grad_h2 = 0.0
+    for j in range(4):
+        wcj = wc[j * width : (j + 1) * width]
+        grad_hidden = jnp.einsum("rd,fd->rf", grad_out, wcj, preferred_element_type=f32)
+        gp = jax.vjp(gelu_tanh, pre[j])[1](grad_hidden)[0].astype(jnp.bfloat16)
+        grad_pre.append(gp)
+        grad_fc1.append(outer(h_second, gp).astype(jnp.bfloat16))
+        grad_h2 = grad_h2 + jnp.einsum("rf,df->rd", gp, wb[j], preferred_element_type=f32)
+    grad_bfc1 = jnp.concatenate([jnp.sum(g.astype(f32), axis=0) for g in grad_pre])
+    second_pull = jax.vjp(modulate, middle, modulation[3], modulation[4])[1]
+    grad_mid_norm, grad_shift_two, grad_scale_two = second_pull(grad_h2)
+    grad_mid = grad_res + grad_mid_norm
+    grad_branch = (modulation[2] * grad_mid).astype(jnp.bfloat16)
+    grad_gate_one = jnp.sum(grad_mid * branch, axis=0)
+    grad_proj = outer(attended, grad_branch).astype(jnp.bfloat16)
+    grad_bproj = jnp.sum(grad_branch.astype(f32), axis=0)
+    grad_att = jnp.einsum("re,de->rd", grad_branch, wa[3], preferred_element_type=f32).astype(jnp.bfloat16)
+    grads = attend_grads(q, k, v, grad_att, length)
+    grad_bqv = [jnp.sum(grads[i].astype(f32), axis=0) for i in (0, 2)]
+    grad_wa = [outer(h_first, g).astype(jnp.bfloat16) for g in grads] + [grad_proj]
+    grad_h1 = sum(jnp.einsum("re,de->rd", g, wa[i], preferred_element_type=f32) for i, g in enumerate(grads))
+    first_pull = jax.vjp(modulate, flat_rows, modulation[0], modulation[1])[1]
+    grad_rows_norm, grad_shift_one, grad_scale_one = first_pull(grad_h1)
+    grad_rows = grad_mid + grad_rows_norm
+    grad_mod = jnp.concatenate(
+        [grad_shift_one, grad_scale_one, grad_gate_one, grad_shift_two, grad_scale_two, grad_gate_two]
+    )
+    out_small = jnp.concatenate(
+        [
+            grad_mod.reshape(8, 864),
+            jnp.concatenate(grad_bqv).reshape(8, 288),
+            grad_bproj.reshape(8, ROWS),
+            grad_bfc1.reshape(8, 576),
+            grad_bfc2.reshape(8, ROWS),
+            jnp.zeros((8, 32), f32),
+        ],
+        axis=1,
+    ).reshape(8, 8, 256)
+    so2, oa, ob, oc = reduce(
+        out_small,
+        jnp.stack(grad_wa).reshape(4, 8, ROWS, width),
+        jnp.stack(grad_fc1).reshape(4, 8, ROWS, width),
+        grad_fc2.reshape(8, 4, ROWS, width),
+    )
+    per_bin = jnp.sum(so2.reshape(4, 8, 2048), axis=1)
+    sums = jnp.sum(per_bin, axis=0)
+    mod_bins = per_bin[:, :864]
+    scaled_bins = lax.all_gather(scaled, "bin", axis=0)
+    grad_wada = jnp.einsum("bd,be->de", scaled_bins.astype(f32), mod_bins, precision=lax.Precision.HIGHEST)
+    mod_mine = lax.dynamic_index_in_dim(mod_bins, lax.axis_index("bin"), 0, keepdims=False)
+    grad_scaled = jnp.sum(w_ada.astype(f32) * mod_mine[None, :], axis=1)
+    grad_scaled = lax.psum(grad_scaled, "fsdp")
+    silu_pull = jax.vjp(jax.nn.silu, cond[0])[1]
+    grad_cond = silu_pull(grad_scaled)[0][None, :]
+    return (
+        block_out.reshape(latents.shape),
+        grad_rows.reshape(latents.shape),
+        grad_cond,
+        grad_wada,
+        sums[:864],
+        jnp.transpose(oa[:3], (1, 0, 2)).reshape(ROWS, 3 * width),
+        sums[864:1152],
+        oa[3],
+        sums[1152:1296],
+        jnp.transpose(ob, (1, 0, 2)).reshape(ROWS, 4 * width),
+        sums[1296:1872],
+        oc.reshape(4 * ROWS, width),
+        sums[1872:2016],
+    )
+
+
 def solution(mesh):
+    fast = mesh.shape["bin"] == 4 and mesh.shape["fsdp"] == 8
     return jax.shard_map(
-        on_device,
+        on_device_fast if fast else on_device_generic,
         mesh=mesh,
         in_specs=(
             P("bin", "fsdp", None, None),

time: 1850 us -> 581 us (0.31)
  waiting for transfers between devices: 1420 us -> 0 us
  Pallas kernels: 0 us -> 336 us
  blocking collectives: 159 us -> 25.7 us
  matrix products: 146 us -> 118 us
    reduce_scatter x4 -> x0, waiting for transfers between devices: 933 us -> none  [the longest x1 351 us: on_device(): lax.psum_scatter(grad_fc1, 'fsdp', scatter_dimension=0, tiled=True)]
    pallas_call x0 -> x4, Pallas kernels: none -> 336 us  [the longest x1 173 us: reduce(): pl.pallas_call(reduce_kernel, out_shape=(jax.ShapeDtypeStruct((32, 8, 256...]
    all_gather x4 -> x0, waiting for transfers between devices: 325 us -> none  [the longest x1 146 us: on_device(): lax.all_gather(w_fc1, 'fsdp', axis=0, tiled=True)]
    psum x1 -> x0, waiting for transfers between devices: 163 us -> none  [on_device(): lax.psum((shards[0], shards[1], shards[2], shards[3], shards[4], shards[5...]
    unnamed x3 -> x0, blocking collectives: 111 us -> none
    dot_general x20 -> x32, matrix products: 146 us -> 118 us  [the longest x9 48.6 us: dense(): return jnp.dot(left, right, preferred_element_type=f32)]
    psum x2 -> x1, blocking collectives: 48.2 us -> 20.5 us  [on_device_fast(): grad_scaled = lax.psum(grad_scaled, 'fsdp')]
    slice x5 -> x11, local copies, waits for them, and re-layouts: 6.18 us -> 29.4 us  [the longest x1 15.4 us: on_device_fast(): wb[j]]
  transfers between devices with their start and end apart: 9 -> 0, of which waited for: 8 -> 0; matrix products, arithmetic and copies ran while one was open for 10% -> 0% of each run, Pallas kernels for 0% -> 0%
where the time goes in v1:
time: 581 us; the launch traced here: 576 us
  Pallas kernels  336 us (58%)
  matrix products  118 us (20%)
  local copies, waits for them, and re-layouts  66.7 us (11%)
  other arithmetic  26.7 us (5%)
  blocking collectives  25.7 us (4%)
    pallas_call x1, Pallas kernels, reduce(): pl.pallas_call(reduce_kernel, out_shape=(jax.ShapeDtypeStruct((32, 8, 256...  173 us
    pallas_call x1, Pallas kernels, gather(): pl.pallas_call(gather_kernel, out_shape=(jax.ShapeDtypeStruct((8, 8, 256)...  145 us
    dot_general x9, matrix products, dense(): return jnp.dot(left, right, preferred_element_type=f32)  48.6 us
    dot_general x9, matrix products, outer(): return jnp.einsum('rd,re->de', left, right, preferred_element_type=f32)  27.3 us
    psum x1, blocking collectives, on_device_fast(): grad_scaled = lax.psum(grad_scaled, 'fsdp')  20.5 us
    dot_general x4, matrix products, on_device_fast(): jnp.einsum('rd,fd->rf', grad_out, wcj, preferred_element_type=f32)  19.7 us
    unnamed x192, local copies, waits for them, and re-layouts  15.8 us
    slice x1, local copies, waits for them, and re-layouts, on_device_fast(): wb[j]  15.4 us

profile of v1, /device:TPU:0, one launch (start us, length us, event | category | flops | bytes accessed | tf_op | source)
XLA Modules:
  0.0 575.8 jit_solution(17495332638361626023)
XLA Ops:
  11.6 145.1 %gather_weights.1 = (f32[8,8,256]{2,1,0:T(8,128)}, bf16[4,8,144,1152]{3,2,1,0:T(8,128)(2,1)}, bf16[4,8,144,1152]{3,2,1,0:T(8,128)(2,1)}, bf16[8,4,144,1152]{3,2,1,0:T(8,128)(2,1)}) custom-call(f32[8,256]{1,0:T(8,128)} %reshape.364.small_ref, bf16[4,144,1152]{2,1,0:T(8,128)(2,1)} %pad_maximum_fusion.3.la_ref, bf16[4,144,1152]{2,1,0:T(8,128)(2,1)} %bitcast.181, ...), custom_call_target="tpu_custom_call" | custom-call | tf_op jit(solution)/shard_map/gather_weights/pallas_call | solution.py:384
  165.2 15.4 %fusion.63 = (bf16[1,8,144,1152]{3,2,1,0:T(8,128)(2,1)}, bf16[1,8,144,1152]{3,2,1,0:T(8,128)(2,1)}, bf16[1,8,144,1152]{3,2,1,0:T(8,128)(2,1)}, bf16[1,8,144,1152...) fusion(bf16[4,8,144,1152]{3,2,1,0:T(8,128)(2,1)} %get-tuple-ele, ...), kind=kLoop, calls=%fused_computation.172 | loop fusion | bytes 42467328 | tf_op jit(solution)/shard_map/slice | solution.py:671
  181.6 3.6 fusion.1.v_ref
  185.9 3.7 fusion.q_ref
  192.7 5.0 attend.1
  201.5 5.7 fusion.61
  212.6 3.9 convolution_add_fusion.6
  216.6 7.6 %fusion.62 = (bf16[2,4,144,1152]{3,2,1,0:T(8,128)(2,1)S(1)}, bf16[2,4,144,1152]{3,2,1,0:T(8,128)(2,1)}, bf16[2,4,144,1152]{3,2,1,0:T(8,128)(2,1)}, bf16[2,4,144,1152]{3,2,1,0:T(8,128)(2,1)}) fusion(bf16[8,4,144,1152]{3,2,1,0:T(8,128)(2,1)} %get-tuple-element.27), kind=kLoop, calls=%fused_computation.171 | loop fusion | bytes 21233664 | tf_op jit(solution)/shard_map/slice | solution.py:687
  224.2 4.9 convert_reduce_fusion.2
  230.5 4.1 convolution_add_fusion.7
  234.6 4.9 convert_reduce_fusion.3
  240.8 4.1 convolution_add_fusion.8
  244.9 4.8 convert_reduce_fusion.4
  251.1 4.1 convolution_add_fusion.9
  255.2 5.1 convert_reduce_fusion.5
  276.4 13.2 %attend_grads.1 = (bf16[512,1152]{1,0:T(8,128)(2,1)S(1)}, bf16[512,1152]{1,0:T(8,128)(2,1)S(1)}, bf16[512,1152]{1,0:T(8,128)(2,1)S(1)}) custom-call(bf16[512,1152]{1,0:T(8,128)(2,1)S(1)} %fusion.q_ref, bf16[512,1152]{1,0:T(8,128)(2,1)S(1)} %convolution_convert_fusion.10.k_ref, bf16[512,1152]{1,0:T(8,128)(2,1)S(1)} %fusion.1.v_ref, ...), custom_call_target="tpu_custom_call" | custom-call | tf_op jit(solution)/shard_map/attend_grads/pallas_call | solution.py:621
  301.9 16.4 %multiply_reduce_fusion.1 = (f32[1152]{0:T(1024)}, f32[1152]{0:T(1024)}, f32[512,1152]{1,0:T(8,128)}, bf16[512,1152]{1,0:T(8,128)(2,1)}, bf16[512,1152]{1,0:T(8,128)(2,1)}, /*index=5*/bf16[512,1152]{1,0:T(8,128)(2,1)}) fusion(bf16[1,2,256,1152]{3,2,1,0:T(8,128)(2,1)} %param.27, f32[512]{0:T(512)} %bitcast.242, f32[512,1152]{1,0:T(8,128)} %get-tuple-element.103, ...), kind=kOutput, calls=%fused_computation.101 | convolution fusion | flops 5471205376 | bytes 33070080 | tf_op jit(solution)/shard_map/dot_general | solution.py:662
  318.3 13.2 %convolution_convert_fusion = bf16[4608,1152]{1,0:T(8,128)(2,1)} fusion(bf16[512,1152]{1,0:T(8,128)(2,1)} %get-tuple-element.84, bf16[512,1152]{1,0:T(8,128)(2,1)} %get-tuple-element.79, bf16[512,1152]{1,0:T(8,128)(2,1)} %get-tuple-element.80, bf16[512,1152]{1,0:T(8,128)(2,1)} %get-tuple-element.81, bf16[512,1152]{1,0:T(8,128)(2,1)} %get-tuple-element.82), kind=kOutput, calls=%fused_computation | convolution fusion | flops 5460000768 | bytes 16515072 | tf_op jit(solution)/shard_map/rd,re->de/dot_general | solution.py:680
  338.8 5.1 pad_maximum_fusion.1.pb_ref
  351.0 5.1 pad_maximum_fusion.pa_ref
  358.3 173.0 %reduce_grads.1 = (f32[32,8,256]{2,1,0:T(8,128)}, f32[4,144,1152]{2,1,0:T(8,128)}, f32[4,144,1152]{2,1,0:T(8,128)}, f32[4,144,1152]{2,1,0:T(8,128)}) custom-call(f32[8,8,256]{2,1,0:T(8,128)} %bitcast.230, bf16[4,8,144,1152]{3,2,1,0:T(8,128)(2,1)} %pad_maximum_fusion.pa_ref, bf16[4,8,144,1152]{3,2,1,0:T(8,128)(2,1)} %pad_maximum_fusion.1.pb_ref, ...), custom_call_target="tpu_custom_call" | custom-call | tf_op jit(solution)/shard_map/reduce_grads/pallas_call | solution.py:531
  532.6 5.2 all-gather
  537.8 3.7 fusion.41
  548.4 20.5 %psum.7 = f32[1152]{0:T(1024)S(1)} all-reduce(f32[1152]{0:T(1024)S(1)} %multiply_reduce_fusion), channel_id=1, replica_groups=mesh['bin'=4,'fsdp'=8] {'fsdp'}, use_global_device_ids=true, to_apply=%region_24.25 | all-reduce | flops 1152 | bytes 9216 | tf_op jit(solution)/shard_map/psum | solution.py:736
  (284 shorter events, 95.7 us)
Async XLA Ops:
  0.6 8.5 %copy-start.42 = (bf16[144,3456]{1,0:T(8,128)(2,1)S(1)}, bf16[144,3456]{1,0:T(8,128)(2,1)}, u32[]{:S(2)}) copy-start(bf16[144,3456]{1,0:T(8,128)(2,1)} %param.19) | copy-start | bytes 2985988
  0.7 8.6 %copy-start.43 = (bf16[144,1152]{1,0:T(8,128)(2,1)S(1)}, bf16[144,1152]{1,0:T(8,128)(2,1)}, u32[]{:S(2)}) copy-start(bf16[144,1152]{1,0:T(8,128)(2,1)} %param.21) | copy-start | bytes 995332
  4.9 5.6 copy-start.32
  11.6 147.5 %copy-start.11 = (bf16[1,2,256,1152]{3,2,1,0:T(8,128)(2,1)S(1)}, bf16[1,2,256,1152]{3,2,1,0:T(8,128)(2,1)}, u32[]{:S(2)}) copy-start(bf16[1,2,256,1152]{3,2,1,0:T(8,128)(2,1)} %param.14) | copy-start | bytes 3538948
  159.1 6.1 %copy-start.49 = (f32[1152]{0:T(1024)}, f32[1152]{0:T(1024)S(1)}, u32[]{:S(2)}) copy-start(f32[1152]{0:T(1024)S(1)} %get-tuple-element.43) | copy-start | bytes 13828
  159.1 6.1 %copy-start.51 = (f32[1152]{0:T(1024)}, f32[1152]{0:T(1024)S(1)}, u32[]{:S(2)}) copy-start(f32[1152]{0:T(1024)S(1)} %get-tuple-element.46) | copy-start | bytes 13828
  165.2 20.6 %copy-start.40 = (bf16[1,2,256,1152]{3,2,1,0:T(8,128)(2,1)}, bf16[1,2,256,1152]{3,2,1,0:T(8,128)(2,1)S(1)}, u32[]{:S(2)}) copy-start(bf16[1,2,256,1152]{3,2,1,0:T(8,128)(2,1)S(1)} %get-tuple-element.111) | copy-start | bytes 3538948
  216.5 7.7 %copy-start.34 = (bf16[1,2,256,1152]{3,2,1,0:T(8,128)(2,1)S(1)}, bf16[1,2,256,1152]{3,2,1,0:T(8,128)(2,1)}, u32[]{:S(2)}) copy-start(bf16[1,2,256,1152]{3,2,1,0:T(8,128)(2,1)} %get-tuple-element.50) | copy-start | bytes 3538948
  255.2 6.2 %copy-start.27 = (bf16[1,8,144,1152]{3,2,1,0:T(8,128)(2,1)S(1)}, bf16[1,8,144,1152]{3,2,1,0:T(8,128)(2,1)}, u32[]{:S(2)}) copy-start(bf16[1,8,144,1152]{3,2,1,0:T(8,128)(2,1)} %get-tuple-element.69) | copy-start | bytes 7962628
  276.4 13.3 %copy-start.22 = (bf16[1,8,144,1152]{3,2,1,0:T(8,128)(2,1)S(1)}, bf16[1,8,144,1152]{3,2,1,0:T(8,128)(2,1)}, u32[]{:S(2)}) copy-start(bf16[1,8,144,1152]{3,2,1,0:T(8,128)(2,1)} %get-tuple-element.107) | copy-start | bytes 7962628
  289.7 5.0 copy-start
  296.9 5.0 copy-start.10
  318.3 13.2 %copy-start.33 = (bf16[512,1152]{1,0:T(8,128)(2,1)S(1)}, bf16[512,1152]{1,0:T(8,128)(2,1)}, u32[]{:S(2)}) copy-start(bf16[512,1152]{1,0:T(8,128)(2,1)} %add_convert_fusion) | copy-start | bytes 3538948
  318.3 13.2 %copy-start.87 = (bf16[512,1152]{1,0:T(8,128)(2,1)S(1)}, bf16[512,1152]{1,0:T(8,128)(2,1)}, u32[]{:S(2)}) copy-start(bf16[512,1152]{1,0:T(8,128)(2,1)} %get-tuple-element.54) | copy-start | bytes 3538948
  338.8 5.1 copy-start.3
  338.8 5.1 copy-start.88
  350.9 5.2 copy-start.74
  350.9 5.3 copy-start.75
  351.0 5.4 copy-start.76
  351.0 5.5 copy-start.77
  358.3 174.2 %copy-start.62 = (bf16[1,1,1152]{2,1,0:T(2,128)(2,1)S(1)}, bf16[1,1,1152]{2,1,0:T(2,128)(2,1)}, u32[]{:S(2)}) copy-start(bf16[1,1,1152]{2,1,0:T(2,128)(2,1)} %get-tuple-element.95) | copy-start | bytes 6916
  531.3 10.2 %copy-start.17 = (f32[4,144,1152]{2,1,0:T(8,128)S(1)}, f32[4,144,1152]{2,1,0:T(8,128)}, u32[]{:S(2)}) copy-start(f32[4,144,1152]{2,1,0:T(8,128)} %get-tuple-element.32) | copy-start | bytes 7962628
  545.9 23.1 %copy-start.46 = (f32[1152]{0:T(1024)S(1)}, f32[1152]{0:T(1024)}, u32[]{:S(2)}) copy-start(f32[1152]{0:T(1024)} %copy-done.45) | copy-start | bytes 13828
  545.9 23.7 %copy-start.41 = (f32[32,8,256]{2,1,0:T(8,128)S(1)}, f32[32,8,256]{2,1,0:T(8,128)}, u32[]{:S(2)}) copy-start(f32[32,8,256]{2,1,0:T(8,128)} %get-tuple-element.31) | copy-start | bytes 786436
  (65 other events, 140.7 us)

commit v2 on v1

--- a/solution.py
+++ b/solution.py
@@ -284,108 +284,397 @@
     )
 
 
+TILE = 256
+STRIP = 16
+
+
 def coords():
-    b=lax.axis_index("bin"); f=lax.axis_index("fsdp")
-    x=b//2; c=lax.rem(b,2); z=f//2; y=lax.rem(f,2)
-    return b,f,x,c,z,y
-
-def gather_kernel(small_ref, la_ref, lb_ref, lc_ref, so_ref, wa_ref, wb_ref, wc_ref, loc_sem, sm_send, sm_recv, send_sem, recv_sem):
-    b,f,x,c,z,y=coords()
-    bx=lax.rem(b+2,4)
-    bc=b+1-2*c
-    bxc=lax.rem(bc+2,4)
-    fy=f+1-2*y
-    z1=z+1-2*lax.rem(z,2)
-    mid=jnp.logical_or(z==1,z==2)
-    zb=lax.rem(z+2,4)
-    zc=3-z
-    z2=jnp.where(mid,zc,zb); z3=jnp.where(mid,zb,zc)
-    bar=pltpu.get_barrier_semaphore()
-    for k in range(1,8):
-        pl.semaphore_signal(bar,inc=1,device_id=(b,lax.rem(f+k,8)),device_id_type=MESH)
-    pl.semaphore_signal(bar,inc=1,device_id=(bx,f),device_id_type=MESH)
-    pl.semaphore_signal(bar,inc=1,device_id=(bc,f),device_id_type=MESH)
-    pl.semaphore_wait(bar,9)
-    W=(wa_ref,wb_ref,wc_ref); L=(la_ref,lb_ref,lc_ref)
-    def blk(g,j,ff):
-        return W[g].at[j,ff] if g<2 else W[g].at[ff,j]
-    smalls=[]
-    for k in range(1,8):
-        cp=pltpu.make_async_remote_copy(src_ref=small_ref,dst_ref=so_ref.at[f],send_sem=sm_send.at[k],recv_sem=sm_recv.at[f],
-            device_id=(b,lax.rem(f+k,8)),device_id_type=MESH)
-        cp.start(); smalls.append(cp)
-    own=pltpu.make_async_copy(small_ref,so_ref.at[f],sm_send.at[0]); own.start()
-    locs=[]
-    for g in range(NG):
-        for j in range(4):
-            cp=pltpu.make_async_copy(L[g].at[j],blk(g,j,f),loc_sem.at[g,j]); cp.start(); locs.append(cp)
-    pend=[]
-    cnt=[0,0,0]
-    def send(g,j,ff,dev,cond=None,src=None):
-        i=cnt[g]; cnt[g]+=1
-        cp=pltpu.make_async_remote_copy(src_ref=blk(g,j,ff) if src is None else src,dst_ref=blk(g,j,ff),send_sem=send_sem.at[g,i],recv_sem=recv_sem.at[g,j,ff],device_id=dev,device_id_type=MESH)
-        if cond is None: cp.start()
+    b = lax.axis_index("bin")
+    f = lax.axis_index("fsdp")
+    return b, f, b // 2, lax.rem(b, 2), f // 2, lax.rem(f, 2)
+
+
+def strip_loop(rows, body):
+    @pl.loop(0, rows // STRIP)
+    def _(k):
+        body(pl.ds(pl.multiple_of(k * STRIP, STRIP), STRIP))
+
+
+def dense(left, right):
+    return jnp.dot(left, right, preferred_element_type=jnp.float32)
+
+
+def dense_nt(left, right):
+    return lax.dot_general(left, right, (((1,), (1,)), ((), ())), preferred_element_type=jnp.float32)
+
+
+def dense_tn(left, right):
+    return lax.dot_general(left, right, (((0,), (0,)), ((), ())), preferred_element_type=jnp.float32)
+
+
+def center_rows(v):
+    v = v - jnp.mean(v, axis=-1, keepdims=True)
+    inv = lax.rsqrt(jnp.mean(v * v, axis=-1, keepdims=True) + 1e-06)
+    return v * inv, inv
+
+
+def head_window(h):
+    start = HEAD_DIM * h
+    low = start // 128 * 128
+    width = 128 if start - low + HEAD_DIM <= 128 else 256
+    return low, width, start - low
+
+
+def head_mask(off, width):
+    lanes = lax.broadcasted_iota(jnp.int32, (1, width), 1)
+    return jnp.logical_and(lanes >= off, lanes < off + HEAD_DIM)
+
+
+def head_probs(q, k):
+    scores = dense_nt(k, q) * HEAD_DIM ** (-0.5)
+    e = jnp.exp(scores - jnp.max(scores, axis=0, keepdims=True))
+    return e * (1.0 / jnp.sum(e, axis=0, keepdims=True))
+
+
+def forward_kernel(
+    vec_ref, la_ref, lb_ref, lc_ref, x_ref, res_ref,
+    vec_out, wa_out, wb_out, wc_out, h1_out, qkv_out, att_out, branch_out, mid_out, h2_out, slope_out, hid_out, go_out, pc_out,
+    wa, wb, wc, vecs, vec, xs, res, h1, qkv, att, mid, h2, hid, go, acc, slope, pst,
+    loc_sem, sm_send, sm_recv, send_sem, recv_sem, in_sem, out_sem, wo_sem, co_sem, sl_sem, ps_sem,
+):
+    b, f, x, c, z, y = coords()
+    bx = lax.rem(b + 2, 4)
+    bc = b + 1 - 2 * c
+    bxc = lax.rem(bc + 2, 4)
+    fy = f + 1 - 2 * y
+    yb = 1 - y
+    z1 = z + 1 - 2 * lax.rem(z, 2)
+    mid_z = jnp.logical_or(z == 1, z == 2)
+    zb = lax.rem(z + 2, 4)
+    zc = 3 - z
+    z2 = jnp.where(mid_z, zc, zb)
+    z3 = jnp.where(mid_z, zb, zc)
+    fz1 = z1 * 2 + y
+    bar = pltpu.get_barrier_semaphore()
+    for k in range(1, 8):
+        pl.semaphore_signal(bar, inc=1, device_id=(b, lax.rem(f + k, 8)), device_id_type=MESH)
+    pl.semaphore_signal(bar, inc=1, device_id=(bx, f), device_id_type=MESH)
+    pl.semaphore_signal(bar, inc=1, device_id=(bc, f), device_id_type=MESH)
+    pl.semaphore_wait(bar, 9)
+
+    W = (wa, wb, wc)
+    L = (la_ref, lb_ref, lc_ref)
+
+    def blk(g, j, ff):
+        if g < 2:
+            return W[g].at[j, pl.ds(pl.multiple_of(ff * ROWS, ROWS), ROWS)]
+        return W[g].at[ff, j]
+
+    smalls = []
+    for k in range(1, 8):
+        cp = pltpu.make_async_remote_copy(
+            src_ref=vec_ref, dst_ref=vecs.at[f], send_sem=sm_send.at[k], recv_sem=sm_recv.at[f],
+            device_id=(b, lax.rem(f + k, 8)), device_id_type=MESH,
+        )
+        cp.start()
+        smalls.append(cp)
+    own = pltpu.make_async_copy(vec_ref, vecs.at[f], sm_send.at[0])
+    own.start()
+
+    pend = []
+    outs = []
+    cnt = [0] * NG
+
+    def send(g, j, ff, dev, cond=None, src=None):
+        i = cnt[g]
+        cnt[g] += 1
+        cp = pltpu.make_async_remote_copy(
+            src_ref=blk(g, j, ff) if src is None else src, dst_ref=blk(g, j, ff),
+            send_sem=send_sem.at[g, i], recv_sem=recv_sem.at[g, j, ff], device_id=dev, device_id_type=MESH,
+        )
+        if cond is None:
+            cp.start()
         else:
             @pl.when(cond)
-            def _(): cp.start()
-        pend.append((cp,cond))
-    def arrive(g,j,ff):
-        pltpu.make_async_copy(blk(g,j,ff),blk(g,j,ff),recv_sem.at[g,j,ff]).wait()
-    up=(b,jnp.minimum(f+2,7)); dn=(b,jnp.maximum(f-2,0))
-    fz1=z1*2+y
+            def _():
+                cp.start()
+        pend.append((cp, cond))
+
+    def copy_out(src, dst, sem):
+        cp = pltpu.make_async_copy(src, dst, sem)
+        cp.start()
+        return cp
+
+    def arrive(g, j, ff, cond=None):
+        def go_on():
+            pltpu.make_async_copy(blk(g, j, ff), blk(g, j, ff), recv_sem.at[g, j, ff]).wait()
+            if g == 2:
+                copy_out(wc.at[ff, j], wc_out.at[ff, j], co_sem.at[j, ff])
+        if cond is None:
+            go_on()
+        else:
+            pl.when(cond)(go_on)
+
+    up = (b, jnp.minimum(f + 2, 7))
+    dn = (b, jnp.maximum(f - 2, 0))
+
     def init(g):
-        sb=L[g].at[b]; sx=L[g].at[bx]
-        send(g,b,f,up,z<3,sb); send(g,b,f,dn,z>0,sb); send(g,b,f,(b,fy),None,sb); send(g,bx,f,(b,fz1),None,sx); send(g,bx,f,(b,fy),None,sx)
-    def Z(g,zz,x_too):
-        ff=zz*2+y
-        arrive(g,b,ff)
-        send(g,b,ff,up,jnp.logical_and(zz<z,z<3)); send(g,b,ff,dn,jnp.logical_and(zz>z,z>0))
-        send(g,b,ff,(b,fy))
-        if x_too: send(g,b,ff,(bx,f))
-        send(g,b,ff,(bc,f))
-    def Y(g,zz,x_too):
-        ff=zz*2+1-y
-        arrive(g,b,ff)
-        if x_too: send(g,b,ff,(bx,f))
-        send(g,b,ff,(bc,f))
-    def X(g,j,ff):
-        arrive(g,j,ff); send(g,j,ff,(bc,f))
-    acts=[]
-    for g in range(NG):
-        a=[lambda g=g: Z(g,z1,False), lambda g=g: X(g,bx,fz1), lambda g=g: Y(g,z,False), lambda g=g: X(g,bx,fy),
-           lambda g=g: Z(g,z2,True), lambda g=g: Y(g,z1,True), lambda g=g: Z(g,z3,True), lambda g=g: X(g,bx,z2*2+y), lambda g=g: Y(g,z2,True),
-           lambda g=g: X(g,bx,z1*2+1-y), lambda g=g: X(g,bx,z3*2+y), lambda g=g: Y(g,z3,True), lambda g=g: X(g,bx,z2*2+1-y), lambda g=g: X(g,bx,z3*2+1-y)]
-        acts.append(a)
+        sb = L[g].at[b]
+        sx = L[g].at[bx]
+        send(g, b, f, up, z < 3, sb)
+        send(g, b, f, dn, z > 0, sb)
+        send(g, b, f, (b, fy), None, sb)
+        send(g, bx, f, (b, fz1), None, sx)
+        send(g, bx, f, (b, fy), None, sx)
+
+    locs = []
+
+    def local(g):
+        for j in range(4):
+            locs.append(copy_out(L[g].at[j], blk(g, j, f), loc_sem.at[g, j]))
+
+    def Z(g, zz, x_too):
+        ff = zz * 2 + y
+        arrive(g, b, ff)
+        send(g, b, ff, up, jnp.logical_and(zz < z, z < 3))
+        send(g, b, ff, dn, jnp.logical_and(zz > z, z > 0))
+        send(g, b, ff, (b, fy))
+        if x_too:
+            send(g, b, ff, (bx, f))
+        send(g, b, ff, (bc, f))
+
+    def Y(g, zz, x_too):
+        ff = zz * 2 + yb
+        arrive(g, b, ff)
+        if x_too:
+            send(g, b, ff, (bx, f))
+        send(g, b, ff, (bc, f))
+
+    def X(g, ff):
+        arrive(g, bx, ff)
+        send(g, bx, ff, (bc, f))
+
+    def actions(g):
+        return [
+            lambda: Z(g, z1, False), lambda: X(g, fz1), lambda: Y(g, z, False), lambda: X(g, fy),
+            lambda: Z(g, z2, True), lambda: Y(g, z1, True), lambda: Z(g, z3, True), lambda: X(g, z2 * 2 + y),
+            lambda: Y(g, z2, True), lambda: X(g, z1 * 2 + yb), lambda: X(g, z3 * 2 + y), lambda: Y(g, z3, True),
+            lambda: X(g, z2 * 2 + yb), lambda: X(g, z3 * 2 + yb),
+        ]
+
+    def other_core(g):
+        for zz in range(4):
+            for jj in (bc, bxc):
+                arrive(g, jj, zz * 2 + y, zz != z)
+                arrive(g, jj, zz * 2 + yb)
+        for cp in locs[g * 4 : g * 4 + 4]:
+            cp.wait()
+
+    def keep(src, dst, i):
+        outs.append(copy_out(src, dst, out_sem.at[i]))
+
+    def row(i):
+        return vec[i : i + 1, :]
+
+    def start_rows():
+        own.wait()
+        for k in range(1, 8):
+            ff = lax.rem(f + k, 8)
+            pltpu.make_async_copy(vecs.at[ff], vecs.at[ff], sm_recv.at[ff]).wait()
+        total = vecs[0]
+        for k in range(1, 8):
+            total = total + vecs[k]
+        vec[...] = total
+        keep(vec, vec_out, 0)
+        in_x.wait()
+
+        def first(r):
+            n, _ = center_rows(xs[r, :].astype(jnp.float32))
+            h1[r, :] = (n * (1.0 + row(1)) + row(0)).astype(jnp.bfloat16)
+
+        strip_loop(h1.shape[0], first)
+        keep(h1, h1_out, 1)
+        in_res.wait()
+
+        def out_grad(r):
+            go[r, :] = (res[r, :].astype(jnp.float32) * row(5)).astype(jnp.bfloat16)
+
+        strip_loop(go.shape[0], out_grad)
+        keep(go, go_out, 2)
+
+    tiles = xs.shape[0] // TILE
+
+    def tile(i):
+        return pl.ds(pl.multiple_of(i * TILE, TILE), TILE)
+
+    def project(j):
+        @pl.loop(0, tiles)
+        def _(i):
+            v = dense(h1[tile(i), :], wa[j])
+            if j != 1:
+                v = v + row(6 + j // 2)
+            qkv[j, tile(i), :] = v.astype(jnp.bfloat16)
+        keep(qkv.at[j], qkv_out.at[j], 3 + j)
+
+    def attention():
+        @pl.loop(0, tiles)
+        def _(i):
+            acc[...] = jnp.zeros_like(acc)
+            for h in range(WID // HEAD_DIM):
+                low, width, off = head_window(h)
+                cols = slice(low, low + width)
+                mask = head_mask(off, width)
+                q = qkv[0, tile(i), cols]
+                v = qkv[2, tile(i), cols]
+                probs = head_probs(jnp.where(mask, q, jnp.zeros_like(q)), qkv[1, tile(i), cols])
+                acc[:, cols] += dense_tn(probs.astype(jnp.bfloat16), jnp.where(mask, v, jnp.zeros_like(v)))
+            att[tile(i), :] = acc[...].astype(jnp.bfloat16)
+        keep(att, att_out, 6)
+
+    def branch():
+        @pl.loop(0, tiles)
+        def _(i):
+            mid[tile(i), :] = dense(att[tile(i), :], wa[3]) + row(8)
+        cp = copy_out(mid, branch_out, out_sem.at[7])
+        cp.wait()
+
+        def second(r):
+            m = xs[r, :].astype(jnp.float32) + row(2) * mid[r, :]
+            mid[r, :] = m
+            n, _ = center_rows(m)
+            h2[r, :] = (n * (1.0 + row(4)) + row(3)).astype(jnp.bfloat16)
+
+        strip_loop(mid.shape[0], second)
+        keep(mid, mid_out, 8)
+        keep(h2, h2_out, 9)
+
+    def hidden(j):
+        cols = slice(j * WID, j * WID + WID)
+
+        @pl.loop(0, tiles)
+        def _(i):
+            acc[...] = dense(h2[tile(i), :], wb[j]) + row(9 + j)
+
+            @pl.when(j * tiles + i >= 1)
+            def _():
+                pltpu.make_async_copy(slope, slope_out.at[tile(0), :WID], sl_sem).wait()
+
+            @pl.loop(0, TILE // STRIP)
+            def _(k):
+                r = pl.ds(pl.multiple_of(k * STRIP, STRIP), STRIP)
+                v = acc[r, :]
+                sq = v * v
+                t = jnp.tanh(0.7978845608028654 * (v + 0.044715 * sq * v))
+                half = 0.5 * (1.0 + t)
+                slope[r, :] = half + 0.5 * v * (1.0 - t * t) * (0.7978845608028654 * (1.0 + 0.134145 * sq))
+                hid[pl.ds(pl.multiple_of(i * TILE + k * STRIP, STRIP), STRIP), cols] = (v * half).astype(jnp.bfloat16)
+
+            copy_out(slope, slope_out.at[tile(i), cols], sl_sem)
+        if j == 3:
+            pltpu.make_async_copy(slope, slope_out.at[tile(0), :WID], sl_sem).wait()
+            keep(hid, hid_out, 10)
+
+    part = pst.shape[1]
+
+    def outer(j):
+        @pl.loop(0, WID // part)
+        def _(i):
+            k = j * (WID // part) + i
+            slot = lax.rem(k, 2)
+
+            @pl.when(k >= 2)
+            def _():
+                pltpu.make_async_copy(pst.at[slot], pc_out.at[pl.ds(0, part)], ps_sem.at[slot]).wait()
+            at = pl.multiple_of(k * part, part)
+            pst[slot] = dense_tn(hid[:, pl.ds(at, part)], go[...]).astype(jnp.bfloat16)
+            copy_out(pst.at[slot], pc_out.at[pl.ds(at, part)], ps_sem.at[slot])
+        if j == 3:
+            for slot in range(2):
+                pltpu.make_async_copy(pst.at[slot], pc_out.at[pl.ds(0, part)], ps_sem.at[slot]).wait()
+
+    def weights_out(g):
+        outs.append(copy_out(W[g], (wa_out, wb_out)[g], wo_sem.at[g]))
+
+    in_x = copy_out(x_ref, xs, in_sem.at[0])
+    in_res = copy_out(res_ref, res, in_sem.at[1])
+    acts = [actions(g) for g in range(NG)]
+    run = lambda todo: [a() for a in todo]
     init(0)
-    for g in range(NG):
-        for i,a in enumerate(acts[g]):
-            a()
-            if i==7 and g<NG-1: init(g+1)
-    for g in range(NG):
-        for zz in range(4):
-            for jj in (bc,bxc):
-                @pl.when(zz!=z)
-                def _(): arrive(g,jj,zz*2+y)
-                arrive(g,jj,zz*2+1-y)
-    for cp,cond in pend:
-        if cond is None: cp.wait_send()
+    local(0)
+    start_rows()
+    run(acts[0][:8])
+    init(1)
+    local(1)
+    run(acts[0][8:])
+    run(acts[1][:5])
+    other_core(0)
+    weights_out(0)
+    work = [lambda: project(0), lambda: project(1), lambda: project(2), attention, branch]
+    ticks = [acts[1][5:6], acts[1][6:7], acts[1][7:8] + [lambda: init(2), lambda: local(2)], acts[1][8:11], acts[1][11:12]]
+    for piece, tick in zip(work, ticks):
+        piece()
+        run(tick)
+    run(acts[1][12:])
+    run(acts[2][:5])
+    other_core(1)
+    weights_out(1)
+    work = [functools.partial(hidden, j) for j in range(4)] + [functools.partial(outer, j) for j in range(4)]
+    ticks = [acts[2][5 + i : 6 + i] for i in range(8)]
+    for piece, tick in zip(work, ticks):
+        piece()
+        run(tick)
+    run(acts[2][13:])
+    for j in range(4):
+        locs[8 + j].wait()
+        copy_out(wc.at[f, j], wc_out.at[f, j], co_sem.at[j, f])
+    other_core_c = 2
+    for zz in range(4):
+        for jj in (bc, bxc):
+            arrive(other_core_c, jj, zz * 2 + y, zz != z)
+            arrive(other_core_c, jj, zz * 2 + yb)
+    for cp, cond in pend:
+        if cond is None:
+            cp.wait_send()
         else:
             @pl.when(cond)
-            def _(cp=cp): cp.wait_send()
-    own.wait()
-    for cp in locs: cp.wait()
-    for cp in smalls: cp.wait_send()
-    for k in range(1,8):
-        ff=lax.rem(f+k,8)
-        pltpu.make_async_copy(so_ref.at[ff],so_ref.at[ff],sm_recv.at[ff]).wait()
-
-def gather(small,la,lb,lc):
-    A=pl.BlockSpec(memory_space=pl.ANY)
-    return pl.pallas_call(gather_kernel,
-        out_shape=(jax.ShapeDtypeStruct((8,8,256),jnp.float32),jax.ShapeDtypeStruct((4,8,ROWS,WID),jnp.bfloat16),jax.ShapeDtypeStruct((4,8,ROWS,WID),jnp.bfloat16),jax.ShapeDtypeStruct((8,4,ROWS,WID),jnp.bfloat16)),
-        in_specs=[A]+[pl.BlockSpec(memory_space=pltpu.VMEM)]*3,out_specs=(A,)*4,
-        scratch_shapes=[pltpu.SemaphoreType.DMA((3,4)),pltpu.SemaphoreType.DMA((8,)),pltpu.SemaphoreType.DMA((8,)),pltpu.SemaphoreType.DMA((3,40)),pltpu.SemaphoreType.DMA((3,4,8))],
-        compiler_params=pltpu.CompilerParams(collective_id=1,has_side_effects=True),name="gather_weights")(small,la,lb,lc)
+            def _(cp=cp):
+                cp.wait_send()
+    for cp in smalls:
+        cp.wait_send()
+    for cp in outs:
+        cp.wait()
+    for ff in range(8):
+        for j in range(4):
+            pltpu.make_async_copy(wc.at[ff, j], wc_out.at[ff, j], co_sem.at[j, ff]).wait()
+
+
+def forward(vec, la, lb, lc, x, res):
+    any_space = pl.BlockSpec(memory_space=pl.ANY)
+    f32, bf16 = jnp.float32, jnp.bfloat16
+    rows = x.shape[0]
+    sds = jax.ShapeDtypeStruct
+    sem = pltpu.SemaphoreType.DMA
+    mat = (rows, WID)
+    outs = (
+        sds((16, WID), f32), sds((4, WID, WID), bf16), sds((4, WID, WID), bf16), sds((8, 4, ROWS, WID), bf16),
+        sds(mat, bf16), sds((3,) + mat, bf16), sds(mat, bf16), sds(mat, f32), sds(mat, f32), sds(mat, bf16),
+        sds((rows, 4 * WID), f32), sds((rows, 4 * WID), bf16), sds(mat, bf16), sds((4 * WID, WID), bf16),
+    )
+    vm = pltpu.VMEM
+    return pl.pallas_call(
+        forward_kernel,
+        out_shape=outs,
+        in_specs=[any_space] * 6,
+        out_specs=(any_space,) * len(outs),
+        scratch_shapes=[
+            vm((4, WID, WID), bf16), vm((4, WID, WID), bf16), vm((8, 4, ROWS, WID), bf16), vm((8, 16, WID), f32), vm((16, WID), f32),
+            vm(mat, bf16), vm(mat, bf16), vm(mat, bf16), vm((3,) + mat, bf16), vm(mat, bf16), vm(mat, f32), vm(mat, bf16),
+            vm((rows, 4 * WID), bf16), vm(mat, bf16), vm((TILE, WID), f32), vm((TILE, WID), f32), vm((2, 384, WID), bf16),
+            sem((NG, 4)), sem((8,)), sem((8,)), sem((NG, 40)), sem((NG, 4, 8)), sem((2,)), sem((12,)), sem((2,)), sem((4, 8)), sem, sem((2,)),
+        ],
+        compiler_params=pltpu.CompilerParams(collective_id=1, has_side_effects=True, vmem_limit_bytes=63 << 20),
+        name="forward",
+    )(vec, la, lb, lc, x, res)
 
 
 def reduce_kernel(small_ref, pa_ref, pb_ref, pc_ref, so_ref, oa_ref, ob_ref, oc_ref,
@@ -536,51 +825,6 @@
         compiler_params=pltpu.CompilerParams(collective_id=2,has_side_effects=True,vmem_limit_bytes=63<<20),name="reduce_grads")(small,pa,pb,pc)
 
 
-def head_window(h):
-    start = HEAD_DIM * h
-    low = start // 128 * 128
-    width = 128 if start - low + HEAD_DIM <= 128 else 256
-    return low, width, start - low
-
-
-def attend_head(q, k, v, off, width):
-    lanes = lax.broadcasted_iota(jnp.int32, (1, width), 1)
-    keep = jnp.logical_and(lanes >= off, lanes < off + HEAD_DIM)
-    q = jnp.where(keep, q, jnp.zeros_like(q))
-    v = jnp.where(keep, v, jnp.zeros_like(v))
-    scores = lax.dot_general(k, q, (((1,), (1,)), ((), ())), preferred_element_type=jnp.float32)
-    scores = scores * HEAD_DIM ** (-0.5)
-    e = jnp.exp(scores - jnp.max(scores, axis=0, keepdims=True))
-    probs = e * (1.0 / jnp.sum(e, axis=0, keepdims=True))
-    return lax.dot_general(
-        probs.astype(jnp.bfloat16), v, (((0,), (0,)), ((), ())), preferred_element_type=jnp.float32
-    )
-
-
-def attend_kernel(q_ref, k_ref, v_ref, out_ref, acc):
-    acc[...] = jnp.zeros_like(acc)
-    for h in range(q_ref.shape[1] // HEAD_DIM):
-        low, width, off = head_window(h)
-        cols = slice(low, low + width)
-        acc[:, cols] += attend_head(q_ref[:, cols], k_ref[:, cols], v_ref[:, cols], off, width)
-    out_ref[...] = acc[...].astype(jnp.bfloat16)
-
-
-def attend(q, k, v, length):
-    rows, width = q.shape
-    spec = pl.BlockSpec((length, width), lambda i: (i, 0))
-    return pl.pallas_call(
-        attend_kernel,
-        grid=(rows // length,),
-        out_shape=jax.ShapeDtypeStruct((rows, width), jnp.bfloat16),
-        in_specs=[spec] * 3,
-        out_specs=spec,
-        scratch_shapes=[pltpu.VMEM((length, width), jnp.float32)],
-        compiler_params=pltpu.CompilerParams(vmem_limit_bytes=40 << 20),
-        name="attend",
-    )(q, k, v)
-
-
 def attend_head_back(q, k, v, g, off, width):
     lanes = lax.broadcasted_iota(jnp.int32, (1, width), 1)
     keep = jnp.logical_and(lanes >= off, lanes < off + HEAD_DIM)
@@ -638,55 +882,44 @@
     f32 = jnp.float32
     scaled = jax.nn.silu(cond[0]).astype(jnp.bfloat16)
     mod_part = jnp.dot(scaled, w_ada, preferred_element_type=f32) + b_ada.astype(f32)
-    biases = jnp.concatenate([b_qv, b_proj, b_fc1, b_fc2]).astype(f32)
-    small = jnp.concatenate([mod_part, biases, jnp.zeros((32,), f32)]).reshape(8, 256)
+    at = lax.axis_index("fsdp")
+
+    def place(part, total):
+        return lax.dynamic_update_slice(jnp.zeros((total,), f32), part, (at * part.shape[0],))
+
+    parts = (mod_part, b_qv.astype(f32), b_proj.astype(f32), b_fc1.astype(f32), b_fc2.astype(f32))
+    vec = jnp.concatenate([place(p, 8 * p.shape[0]) for p in parts] + [jnp.zeros((2 * width,), f32)]).reshape(16, width)
     la = jnp.concatenate([jnp.transpose(w_qkv.reshape(ROWS, 3, WID), (1, 0, 2)), w_proj[None]])
     lb = jnp.transpose(w_fc1.reshape(ROWS, 4, WID), (1, 0, 2))
     lc = w_fc2.reshape(4, ROWS, WID)
-    so, wa, wb, wc = gather(small, la, lb, lc)
-    so = so.reshape(8, 2048)
-    modulation = so[:, :864].reshape(6, width)
-    bias_qv = so[:, 864:1152].reshape(2, width)
-    bias_proj = so[:, 1152:1296].reshape(width)
-    bias_fc1 = so[:, 1296:1872].reshape(4 * width)
-    bias_fc2 = so[:, 1872:2016].reshape(width)
-    wa = wa.reshape(4, width, width)
-    wb = wb.reshape(4, width, width)
-    wc = wc.reshape(4 * width, width)
-    flat_rows = latents[0].reshape(rows, width).astype(f32)
     live_mask = (lax.iota(jnp.int32, images) < live[0, 0]).astype(f32)
     row_mask = jnp.repeat(live_mask, length)[:, None]
-    h_first = modulate(flat_rows, modulation[0], modulation[1]).astype(jnp.bfloat16)
-
-    def dense(left, right):
+    x_rows = latents[0].reshape(rows, width)
+    res = cotangent[0].reshape(rows, width) * row_mask.astype(jnp.bfloat16)
+    vec, wa, wb, wc, h_first, qkv, attended, branch, middle, h_second, slope, hidden, grad_out, grad_fc2 = forward(vec, la, lb, lc, x_rows, res)
+    modulation = vec[:6]
+    bias_fc2 = vec[13]
+    wc = wc.reshape(4 * width, width)
+    flat_rows = x_rows.astype(f32)
+
+    def dense_x(left, right):
         return jnp.dot(left, right, preferred_element_type=f32)
 
-    q = (dense(h_first, wa[0]) + bias_qv[0]).astype(jnp.bfloat16)
-    k = dense(h_first, wa[1]).astype(jnp.bfloat16)
-    v = (dense(h_first, wa[2]) + bias_qv[1]).astype(jnp.bfloat16)
-    attended = attend(q, k, v, length)
-    branch = dense(attended, wa[3]) + bias_proj
-    middle = flat_rows + modulation[2] * branch
-    h_second = modulate(middle, modulation[3], modulation[4]).astype(jnp.bfloat16)
-    pre = [dense(h_second, wb[j]) + bias_fc1[j * width : (j + 1) * width] for j in range(4)]
-    hidden = jnp.concatenate([gelu_tanh(p).astype(jnp.bfloat16) for p in pre], axis=1)
-    mlp_out = dense(hidden, wc) + bias_fc2
+    mlp_out = dense_x(hidden, wc) + bias_fc2
     block_out = ((middle + modulation[5] * mlp_out) * row_mask).astype(jnp.bfloat16)
-    grad_res = cotangent[0].reshape(rows, width).astype(f32) * row_mask
-    grad_out = (modulation[5] * grad_res).astype(jnp.bfloat16)
+    grad_res = res.astype(f32)
     grad_gate_two = jnp.sum(grad_res * mlp_out, axis=0)
 
     def outer(left, right):
         return jnp.einsum("rd,re->de", left, right, preferred_element_type=f32)
 
-    grad_fc2 = outer(hidden, grad_out).astype(jnp.bfloat16)
     grad_bfc2 = jnp.sum(grad_out.astype(f32), axis=0)
     grad_pre, grad_fc1 = [], []
     grad_h2 = 0.0
     for j in range(4):
         wcj = wc[j * width : (j + 1) * width]
         grad_hidden = jnp.einsum("rd,fd->rf", grad_out, wcj, preferred_element_type=f32)
-        gp = jax.vjp(gelu_tanh, pre[j])[1](grad_hidden)[0].astype(jnp.bfloat16)
+        gp = (grad_hidden * slope[:, j * width : (j + 1) * width]).astype(jnp.bfloat16)
         grad_pre.append(gp)
         grad_fc1.append(outer(h_second, gp).astype(jnp.bfloat16))
         grad_h2 = grad_h2 + jnp.einsum("rf,df->rd", gp, wb[j], preferred_element_type=f32)
@@ -699,7 +932,7 @@
     grad_proj = outer(attended, grad_branch).astype(jnp.bfloat16)
     grad_bproj = jnp.sum(grad_branch.astype(f32), axis=0)
     grad_att = jnp.einsum("re,de->rd", grad_branch, wa[3], preferred_element_type=f32).astype(jnp.bfloat16)
-    grads = attend_grads(q, k, v, grad_att, length)
+    grads = attend_grads(qkv[0], qkv[1], qkv[2], grad_att, length)
     grad_bqv = [jnp.sum(grads[i].astype(f32), axis=0) for i in (0, 2)]
     grad_wa = [outer(h_first, g).astype(jnp.bfloat16) for g in grads] + [grad_proj]
     grad_h1 = sum(jnp.einsum("re,de->rd", g, wa[i], preferred_element_type=f32) for i, g in enumerate(grads))

time: 581 us -> 544 us (0.936)
  matrix products: 118 us -> 78.6 us
  local copies, waits for them, and re-layouts: 66.7 us -> 53.1 us
  Pallas kernels: 336 us -> 348 us
    dot_general x9 -> x1, matrix products: 48.6 us -> 11.3 us  [dense_x(): return jnp.dot(left, right, preferred_element_type=f32)]
    slice x5 -> x0, local copies, waits for them, and re-layouts: 19.2 us -> none  [the longest x1 15.4 us: on_device_fast(): wb[j]]
    pallas_call x2 -> x1, Pallas kernels: 150 us -> 162 us  [forward(): pl.pallas_call(forward_kernel, out_shape=outs, in_specs=[any_space] * 6,...]
    dot_general x9 -> x8, matrix products: 27.3 us -> 16.7 us  [outer(): return jnp.einsum('rd,re->de', left, right, preferred_element_type=f32)]
    add x8 -> x0, local copies, waits for them, and re-layouts: 8.95 us -> none  [the longest x4 5.45 us: on_device_fast(): dense(h_second, wb[j]) + bias_fc1[j * width:(j + 1) * width]]
    unnamed x192 -> x162, local copies, waits for them, and re-layouts: 15.8 us -> 19.6 us
where the time goes in v2:
time: 544 us; the launch traced here: 540 us
  Pallas kernels  348 us (64%)
  matrix products  78.6 us (14%)
  local copies, waits for them, and re-layouts  53.1 us (10%)
  other arithmetic  31 us (6%)
  blocking collectives  26.7 us (5%)
    pallas_call x1, Pallas kernels, reduce(): pl.pallas_call(reduce_kernel, out_shape=(jax.ShapeDtypeStruct((32, 8, 256...  172 us
    pallas_call x1, Pallas kernels, forward(): pl.pallas_call(forward_kernel, out_shape=outs, in_specs=[any_space] * 6,...  162 us
    dot_general x4, matrix products, on_device_fast(): jnp.einsum('rd,fd->rf', grad_out, wcj, preferred_element_type=f32)  23.2 us
    psum x1, blocking collectives, on_device_fast(): grad_scaled = lax.psum(grad_scaled, 'fsdp')  20.1 us
    unnamed x162, local copies, waits for them, and re-layouts  19.6 us
    dot_general x8, matrix products, outer(): return jnp.einsum('rd,re->de', left, right, preferred_element_type=f32)  16.7 us
    pallas_call x1, Pallas kernels, attend_grads(): pl.pallas_call(attend_back_kernel, grid=(rows // length,), out_shape=(jax...  13.5 us
    dot_general x4, matrix products, on_device_fast(): jnp.einsum('rf,df->rd', gp, wb[j], preferred_element_type=f32)  13 us

profile of v2, /device:TPU:0, one launch (start us, length us, event | category | flops | bytes accessed | tf_op | source)
XLA Modules:
  0.0 539.8 jit_solution(4103696850056989069)
XLA Ops:
  7.7 6.6 %all-gather = bf16[4,1,1152]{2,1,0:T(2,128)(2,1)} all-gather(bf16[1,1,1152]{2,1,0:T(2,128)(2,1)S(1)} %get-tuple-element.83), channel_id=1, replica_groups=mesh['bin'=4,'fsdp'=8] {'bin'}, dimensions={0}, use_global_device_ids=true | all-gather | bytes 11520 | tf_op jit(solution)/shard_map/all_gather | solution.py:965
  19.3 161.9 %forward.1 = (f32[16,1152]{1,0:T(8,128)}, bf16[4,1152,1152]{2,1,0:T(8,128)(2,1)}, bf16[4,1152,1152]{2,1,0:T(8,128)(2,1)}, bf16[8,4,144,1152]{3,2,1,0:T(8,128)(2,...) custom-call(f32[16,1152]{1,0:T(8,128)} %reshape.194.vec_ref, ...), custom_call_target="tpu_custom_call" | custom-call | tf_op jit(solution)/shard_map/forward/pallas_call | solution.py:664
  187.8 2.3 slice_bitcast_fusion.1
  190.0 7.3 %fusion.35 = (bf16[2,4,144,1152]{3,2,1,0:T(8,128)(2,1)S(1)}, bf16[2,4,144,1152]{3,2,1,0:T(8,128)(2,1)}, bf16[2,4,144,1152]{3,2,1,0:T(8,128)(2,1)}, bf16[2,4,144,1152]{3,2,1,0:T(8,128)(2,1)}) fusion(bf16[8,4,144,1152]{3,2,1,0:T(8,128)(2,1)} %get-tuple-element.37), kind=kLoop, calls=%fused_computation.132 | loop fusion | bytes 21233664 | tf_op jit(solution)/shard_map/slice | solution.py:920
  197.4 5.2 convert_reduce_fusion.2
  204.0 6.4 %convert_reduce_fusion.3 = (f32[1152]{0:T(1024)}, bf16[512,1152]{1,0:T(8,128)(2,1)}) fusion(f32[512,4608]{1,0:T(8,128)} %get-tuple-element.39, bf16[512,1152]{1,0:T(8,128)(2,1)} %get-tuple-element.38, bf16[1152,1152]{1,0:T(8,128)(2,1)} %bitcast.159), kind=kOutput, calls=%fused_computation.55 | convolution fusion | flops 1361312640 | bytes 7377408 | tf_op jit(solution)/shard_map/rd,fd->rf/dot_general | solution.py:921
  211.7 6.4 %convert_reduce_fusion.4 = (f32[1152]{0:T(1024)}, bf16[512,1152]{1,0:T(8,128)(2,1)}) fusion(f32[512,4608]{1,0:T(8,128)} %get-tuple-element.39, bf16[512,1152]{1,0:T(8,128)(2,1)} %get-tuple-element.38, bf16[1152,1152]{1,0:T(8,128)(2,1)} %bitcast.158), kind=kOutput, calls=%fused_computation.56 | convolution fusion | flops 1361312640 | bytes 7377408 | tf_op jit(solution)/shard_map/rd,fd->rf/dot_general | solution.py:921
  218.1 5.2 convert_reduce_fusion.5
  227.4 4.1 fusion.12
  231.6 4.2 convolution_add_fusion.5
  237.8 2.9 multiply_reduce_fusion.1
  244.3 4.0 convolution_convert_fusion.8.g_ref
  248.3 13.5 %attend_grads.1 = (bf16[512,1152]{1,0:T(8,128)(2,1)S(1)}, bf16[512,1152]{1,0:T(8,128)(2,1)S(1)}, bf16[512,1152]{1,0:T(8,128)(2,1)S(1)}) custom-call(bf16[512,1152]{1,0:T(8,128)(2,1)S(1)} %get-tuple-element.79.q_ref, bf16[512,1152]{1,0:T(8,128)(2,1)S(1)} %get-tuple-element.78.k_ref, bf16[512,1152]{1,0:T(8,128)(2,1)S(1)} %get-tuple-element.77.v_ref, ...), custom_call_target="tpu_custom_call" | custom-call | tf_op jit(solution)/shard_map/attend_grads/pallas_call | solution.py:865
  267.2 3.2 convolution_convert_fusion.4
  277.6 5.7 %pad_maximum_fusion.1.pb_ref = bf16[4,8,144,1152]{3,2,1,0:T(8,128)(2,1)} fusion(bf16[1,8,144,1152]{3,2,1,0:T(8,128)(2,1)S(1)} %bitcast.160, bf16[1,8,144,1152]{3,2,1,0:T(8,128)(2,1)S(1)} %bitcast.161, bf16[1,8,144,1152]{3,2,1,0:T(8,128)(2,1)S(1)} %bitcast.164, bf16[1,8,144,1152]{3,2,1,0:T(8,128)(2,1)S(1)} %bitcast.166), kind=kLoop, calls=%fused_computation.1 | loop fusion | flops 15925248 | bytes 21233664 | tf_op jit(solution)/shard_map/stack | solution.py:959
  288.4 2.2 multiply_reduce_fusion.4
  295.9 11.3 %fusion.22 = (f32[1152]{0:T(1024)S(1)}, f32[1152]{0:T(1024)S(1)}, f32[512,1152]{1,0:T(8,128)}, bf16[512,1152]{1,0:T(8,128)(2,1)}) fusion(bf16[512,1152]{1,0:T(8,128)(2,1)} %bitcast_multiply_fusion.res_ref, f32[512,1152]{1,0:T(8,128)} %get-tuple-element.46, f32[512,1152]{1,0:T(8,128)S(1)} %copy-done.11, f32[512]{0:T(512)S(1)} %copy-done.39, ...), kind=kOutput, calls=%fused_computation.50 | convolution fusion | flops 5448202240 | bytes 30706176 | tf_op jit(solution)/shard_map/dot_general | solution.py:906
  317.5 3.1 convolution_convert_fusion.5
  324.1 5.1 pad_maximum_fusion.pa_ref
  329.3 172.3 %reduce_grads.1 = (f32[32,8,256]{2,1,0:T(8,128)}, f32[4,144,1152]{2,1,0:T(8,128)}, f32[4,144,1152]{2,1,0:T(8,128)}, f32[4,144,1152]{2,1,0:T(8,128)}) custom-call(f32[8,8,256]{2,1,0:T(8,128)} %bitcast.173, bf16[4,8,144,1152]{3,2,1,0:T(8,128)(2,1)} %pad_maximum_fusion.pa_ref, bf16[4,8,144,1152]{3,2,1,0:T(8,128)(2,1)} %pad_maximum_fusion.1.pb_ref, ...), custom_call_target="tpu_custom_call" | custom-call | tf_op jit(solution)/shard_map/reduce_grads/pallas_call | solution.py:820
  501.6 3.7 copy.39
  508.5 20.1 %psum.7 = f32[1152]{0:T(1024)S(1)} all-reduce(f32[1152]{0:T(1024)S(1)} %multiply_reduce_fusion), channel_id=1, replica_groups=mesh['bin'=4,'fsdp'=8] {'fsdp'}, use_global_device_ids=true, to_apply=%region_24.25 | all-reduce | flops 1152 | bytes 9216 | tf_op jit(solution)/shard_map/psum | solution.py:969
  529.2 2.0 slice_bitcast_fusion.4
  534.3 3.7 fusion.25
  (243 shorter events, 74.8 us)
Async XLA Ops:
  0.6 6.4 %copy-start.12 = (bf16[1152,864]{0,1:T(8,128)(2,1)S(1)}, bf16[1152,864]{0,1:T(8,128)(2,1)}, u32[]{:S(2)}) copy-start(bf16[1152,864]{0,1:T(8,128)(2,1)} %param.17) | copy-start | bytes 5971972
  0.7 6.1 %copy-start.53 = (bf16[144]{0:T(256)(128)(2,1)S(1)}, bf16[144]{0:T(256)(128)(2,1)}, u32[]{:S(2)}) copy-start(bf16[144]{0:T(256)(128)(2,1)} %param.26) | copy-start | bytes 868
  0.7 13.7 %copy-start.49 = (bf16[576]{0:T(1024)(128)(2,1)S(1)}, bf16[576]{0:T(1024)(128)(2,1)}, u32[]{:S(2)}) copy-start(bf16[576]{0:T(1024)(128)(2,1)} %param.24) | copy-start | bytes 3460
  0.7 6.2 %copy-start.51 = (bf16[288]{0:T(512)(128)(2,1)S(1)}, bf16[288]{0:T(512)(128)(2,1)}, u32[]{:S(2)}) copy-start(bf16[288]{0:T(512)(128)(2,1)} %param.20) | copy-start | bytes 1732
  0.7 13.8 %copy-start.50 = (bf16[864]{0:T(1024)(128)(2,1)S(1)}, bf16[864]{0:T(1024)(128)(2,1)}, u32[]{:S(2)}) copy-start(bf16[864]{0:T(1024)(128)(2,1)} %param.18) | copy-start | bytes 5188
  0.7 6.3 %copy-start.48 = (f32[1,1152]{1,0:T(1,128)S(1)}, f32[1,1152]{1,0:T(1,128)}, u32[]{:S(2)}) copy-start(f32[1,1152]{1,0:T(1,128)} %param.15) | copy-start | bytes 13828
  2.2 14.4 %copy-start.35 = (bf16[512]{0:T(512)(128)(2,1)}, bf16[512]{0:T(512)(128)(2,1)S(1)}, u32[]{:S(2)}) copy-start(bf16[512]{0:T(512)(128)(2,1)S(1)} %convert_element_type.122) | copy-start | bytes 3076
  2.2 13.1 %copy-start.25 = (bf16[144,3456]{1,0:T(8,128)(2,1)S(1)}, bf16[144,3456]{1,0:T(8,128)(2,1)}, u32[]{:S(2)}) copy-start(bf16[144,3456]{1,0:T(8,128)(2,1)} %param.19) | copy-start | bytes 2985988
  5.5 9.9 %copy-start.26 = (bf16[144,1152]{1,0:T(8,128)(2,1)S(1)}, bf16[144,1152]{1,0:T(8,128)(2,1)}, u32[]{:S(2)}) copy-start(bf16[144,1152]{1,0:T(8,128)(2,1)} %param.21) | copy-start | bytes 995332
  190.0 7.4 %copy-start.21 = (bf16[512,1152]{1,0:T(8,128)(2,1)S(1)}, bf16[512,1152]{1,0:T(8,128)(2,1)}, u32[]{:S(2)}) copy-start(bf16[512,1152]{1,0:T(8,128)(2,1)} %get-tuple-element.38) | copy-start | bytes 3538948
  211.7 6.4 %copy-start.18 = (bf16[2,4,144,1152]{3,2,1,0:T(8,128)(2,1)S(1)}, bf16[2,4,144,1152]{3,2,1,0:T(8,128)(2,1)}, u32[]{:S(2)}) copy-start(bf16[2,4,144,1152]{3,2,1,0:T(8,128)(2,1)} %get-tuple-element.75) | copy-start | bytes 7962628
  211.7 6.4 %copy-start.22 = (bf16[512,1152]{1,0:T(8,128)(2,1)S(1)}, bf16[512,1152]{1,0:T(8,128)(2,1)}, u32[]{:S(2)}) copy-start(bf16[512,1152]{1,0:T(8,128)(2,1)} %get-tuple-element.38) | copy-start | bytes 3538948
  227.4 8.3 %slice-start.6 = ((s8[10616832]{0:T(1024)(128)(4,1)}), s8[4194304]{0:T(1024)(128)(4,1)S(1)}, s32[]{:S(2)}) async-start(s8[10616832]{0:T(1024)(128)(4,1)} %bitcast.188), calls=%async_computation.6 | async-start | bytes 8388608
  227.4 8.3 %slice-start.7 = ((s8[10616832]{0:T(1024)(128)(4,1)}), s8[4194304]{0:T(1024)(128)(4,1)S(1)}, s32[]{:S(2)}) async-start(s8[10616832]{0:T(1024)(128)(4,1)} %bitcast.188), calls=%async_computation.7 | async-start | bytes 8388608
  275.8 7.4 %slice-start.3 = ((s8[10616832]{0:T(1024)(128)(4,1)}), s8[4194304]{0:T(1024)(128)(4,1)S(1)}, s32[]{:S(2)}) async-start(s8[10616832]{0:T(1024)(128)(4,1)} %bitcast.186), calls=%async_computation.3 | async-start | bytes 8388608
  277.5 6.9 %slice-start.5 = ((s8[10616832]{0:T(1024)(128)(4,1)}), s8[2228224]{0:T(1024)(128)(4,1)S(1)}, s32[]{:S(2)}) async-start(s8[10616832]{0:T(1024)(128)(4,1)} %bitcast.186), calls=%async_computation.5 | async-start | bytes 4456448
  286.4 9.4 %slice-start = ((s8[10616832]{0:T(1024)(128)(4,1)}), s8[4194304]{0:T(1024)(128)(4,1)S(1)}, s32[]{:S(2)}) async-start(s8[10616832]{0:T(1024)(128)(4,1)} %bitcast.147), calls=%async_computation | async-start | bytes 8388608
  286.4 9.4 %slice-start.1 = ((s8[10616832]{0:T(1024)(128)(4,1)}), s8[4194304]{0:T(1024)(128)(4,1)S(1)}, s32[]{:S(2)}) async-start(s8[10616832]{0:T(1024)(128)(4,1)} %bitcast.147), calls=%async_computation.1 | async-start | bytes 8388608
  288.4 7.4 %slice-start.2 = ((s8[10616832]{0:T(1024)(128)(4,1)}), s8[2228224]{0:T(1024)(128)(4,1)S(1)}, s32[]{:S(2)}) async-start(s8[10616832]{0:T(1024)(128)(4,1)} %bitcast.147), calls=%async_computation.2 | async-start | bytes 4456448
  288.4 7.4 %copy-start.11 = (f32[512,1152]{1,0:T(8,128)S(1)}, f32[512,1152]{1,0:T(8,128)}, u32[]{:S(2)}) copy-start(f32[512,1152]{1,0:T(8,128)} %copy-done.10) | copy-start | bytes 7077892
  295.9 12.7 %copy-start.42 = (f32[1152]{0:T(1024)S(1)}, f32[1152]{0:T(1024)}, u32[]{:S(2)}) copy-start(f32[1152]{0:T(1024)} %get-tuple-element.59) | copy-start | bytes 13828
  295.9 14.0 %copy-start.41 = (f32[1152]{0:T(1024)S(1)}, f32[1152]{0:T(1024)}, u32[]{:S(2)}) copy-start(f32[1152]{0:T(1024)} %get-tuple-element.55) | copy-start | bytes 13828
  295.9 18.6 %copy-start.30 = (f32[8,144]{1,0:T(8,128)S(1)}, f32[8,144]{1,0:T(8,128)}, u32[]{:S(2)}) copy-start(f32[8,144]{1,0:T(8,128)} %reshape.203) | copy-start | bytes 13828
  501.6 6.5 %copy-start.13 = (bf16[1152,864]{0,1:T(8,128)(2,1)S(1)}, bf16[1152,864]{0,1:T(8,128)(2,1)}, u32[]{:S(2)}) copy-start(bf16[1152,864]{0,1:T(8,128)(2,1)} %param.17) | copy-start | bytes 5971972
  (48 other events, 130.4 us)
